TPU v7x, 32 devices: a whole 2x2x4 slice. The times are simulated.
32 devices in a mesh: batch: 2 (over x), ctx: 16 (over z, y, core).
Axes of the slice: x: 2, y: 2, z: 4, core: 2. Of those that a mesh axis runs over, the one named last changes fastest.
Arguments:
- layer_input: bfloat16 [4, 2, 1536, 768], P('batch', None, 'ctx'), may hold values from -6 to 6
- cotangent: bfloat16 [4, 2, 1536, 768], P('batch', None, 'ctx'), may hold values from -6 to 6
- prefix: int32 [4], P('batch'), may hold values from 153 to 768, as said below
- block_size: int32 [4], P('batch'), may hold values from 4 to 16, as said below
- ln1_gain: bfloat16 [768], P(('batch', 'ctx')), may hold values from 0.5 to 1.5
- ln1_bias: bfloat16 [768], P(('batch', 'ctx')), may hold values from -1.75 to 1.75
- qkv_weight: bfloat16 [768, 2304], P(('batch', 'ctx')), may hold values from -0.21875 to 0.21875
- qkv_bias: bfloat16 [2304], P(('batch', 'ctx')), may hold values from -0.1875 to 0.1875
- out_weight: bfloat16 [768, 768], P(('batch', 'ctx')), may hold values from -0.625 to 0.625
- out_bias: bfloat16 [768], P(('batch', 'ctx')), may hold values from -0.625 to 0.625
- ln2_gain: bfloat16 [768], P(('batch', 'ctx')), may hold values from 0.5 to 1.5
- ln2_bias: bfloat16 [768], P(('batch', 'ctx')), may hold values from -1.75 to 1.75
- up_weight: bfloat16 [768, 3072], P(('batch', 'ctx')), may hold values from -0.21875 to 0.21875
- up_bias: bfloat16 [3072], P(('batch', 'ctx')), may hold values from -1.75 to 1.75
- down_weight: bfloat16 [3072, 768], P(('batch', 'ctx')), may hold values from -0.109375 to 0.109375
- down_bias: bfloat16 [768], P(('batch', 'ctx')), may hold values from -1.75 to 1.75
Outputs:
- block_out: bfloat16 [4, 2, 1536, 768], P('batch', None, 'ctx')
- grad_input: bfloat16 [4, 2, 1536, 768], P('batch', None, 'ctx')
- grad_ln1_gain: float32 [768], P(('batch', 'ctx'))
- grad_ln1_bias: float32 [768], P(('batch', 'ctx'))
- grad_qkv_weight: float32 [768, 2304], P(('batch', 'ctx'))
- grad_qk_bias: float32 [1536], P(('batch', 'ctx'))
- grad_value_bias: float32 [768], P(('batch', 'ctx'))
- grad_out_weight: float32 [768, 768], P(('batch', 'ctx'))
- grad_out_bias: float32 [768], P(('batch', 'ctx'))
- grad_ln2_gain: float32 [768], P(('batch', 'ctx'))
- grad_ln2_bias: float32 [768], P(('batch', 'ctx'))
- grad_up_weight: float32 [768, 3072], P(('batch', 'ctx'))
- grad_up_bias: float32 [3072], P(('batch', 'ctx'))
- grad_down_weight: float32 [3072, 768], P(('batch', 'ctx'))
- grad_down_bias: float32 [768], P(('batch', 'ctx'))
Inputs may be any that keep to these rules, and one draw needn't show every extreme that they name: `prefix`: per sequence, from a tenth to a half of 1536; in every draw some sequence has exactly 153 and some exactly 768. `block_size`: each value is 4, 8 or 16, and all three occur in every draw.
All inputs are finite; a program needn't handle non-finite values.
Results may differ from a plain program's by a relative error of at most 0.019.
Values may be sent and summed in bfloat16 or wider, within the bound.
No kernel may reach another device: no remote copies, remote signals or barrier semaphores. Data moves between devices by JAX's collectives and lax.ppermute only.
A program may use at most 256 MiB of HBM per device.

v0:
```python
import jax
import jax.numpy as jnp
from jax import lax
from jax.sharding import PartitionSpec as P

HEADS = 12
HEAD_DIM = 64


SCALE = 0.125
NEGATIVE = -1e30
EPSILON = 1e-05
THETA = 10000.0
BLOCK_LIMIT = 768


def layer_norm(values, gain_vec, bias_add):
    center = values - jnp.mean(values, -1, keepdims=True)
    spread = jnp.mean(center * center, -1, keepdims=True)
    return center * lax.rsqrt(spread + EPSILON) * gain_vec + bias_add


def rotary_tables(positions):
    half_dim = HEAD_DIM // 2
    inverse = 1.0 / THETA ** (jnp.arange(half_dim, dtype=jnp.float32) / half_dim)
    angles = positions.astype(jnp.float32)[:, None] * inverse[None, :]
    return (jnp.cos(angles)[:, None, :], jnp.sin(angles)[:, None, :])


def rotate(values, cos_tab, sin_tab):
    half_dim = values.shape[-1] // 2
    first_half = values[..., :half_dim]
    second = values[..., half_dim:]
    return jnp.concatenate(
        [first_half * cos_tab - second * sin_tab, second * cos_tab + first_half * sin_tab], -1
    )


def block_length(piece_rows):
    for pieces in range(1, piece_rows + 1):
        if piece_rows % pieces == 0 and piece_rows // pieces <= BLOCK_LIMIT:
            return piece_rows // pieces
    return piece_rows


def clean_allowed(query_copy, query_pos, key_pos, prefix_len, block_len):
    query_block = (query_pos // block_len)[:, None]
    key_block = (key_pos // block_len)[None, :]
    query_at = query_pos[:, None]
    key_at = key_pos[None, :]
    for_noisy = (key_block < query_block) | (key_at < prefix_len)
    for_clean = (query_at < prefix_len) & (key_at < prefix_len) | (query_at >= prefix_len) & (
        key_block <= query_block
    )
    return jnp.where((query_copy == 0)[:, None], for_noisy, for_clean)


def absorb(running, query_rows, key_rows, value_rows, allowed):
    row_best, row_total, weighted = running
    scores = (
        jnp.einsum("rhd,khd->rhk", query_rows, key_rows, preferred_element_type=jnp.float32) * SCALE
    )
    scores = jnp.where(allowed, scores, NEGATIVE)
    new_best = jnp.maximum(row_best, jnp.max(scores, -1))
    weights = jnp.where(allowed, jnp.exp(scores - new_best[..., None]), 0.0)
    factor = jnp.exp(row_best - new_best)
    row_total = row_total * factor + jnp.sum(weights, -1)
    weighted = weighted * factor[..., None] + jnp.einsum(
        "rhk,khd->rhd", weights.astype(jnp.bfloat16), value_rows, preferred_element_type=jnp.float32
    )
    return (new_best, row_total, weighted)


def score_grads(query_rows, grad_rows, log_total, row_delta, key_rows, value_rows, allowed):
    scores = (
        jnp.einsum("rhd,khd->rhk", query_rows, key_rows, preferred_element_type=jnp.float32) * SCALE
    )
    scores = jnp.where(allowed, scores, NEGATIVE)
    prob_full = jnp.where(allowed, jnp.exp(scores - log_total[..., None]), 0.0)
    grad_prob = jnp.einsum(
        "rhd,khd->rhk", grad_rows, value_rows, preferred_element_type=jnp.float32
    )
    grad_score = (prob_full * (grad_prob - row_delta[..., None]) * SCALE).astype(jnp.bfloat16)
    return (prob_full.astype(jnp.bfloat16), grad_score)


def take_rows(array, block_index, length):
    return lax.dynamic_slice_in_dim(array, block_index * length, length, 1)


def on_device(
    layer_input,
    cotangent,
    prefix,
    block_size,
    ln1_gain,
    ln1_bias,
    qkv_weight,
    qkv_bias,
    out_weight,
    out_bias,
    ln2_gain,
    ln2_bias,
    up_weight,
    up_bias,
    down_weight,
    down_bias,
):
    shard_list = (
        ln1_gain,
        ln1_bias,
        qkv_weight,
        qkv_bias,
        out_weight,
        out_bias,
        ln2_gain,
        ln2_bias,
        up_weight,
        up_bias,
        down_weight,
        down_bias,
    )
    all_devices = lax.axis_size("batch") * lax.axis_size("ctx")
    micro_count = layer_input.shape[0]
    pos_dev = layer_input.shape[2]
    width = layer_input.shape[3]
    row_count = 2 * pos_dev
    positions = lax.axis_index("ctx") * pos_dev + jnp.arange(pos_dev, dtype=jnp.int32)
    row_pos = jnp.concatenate([positions, positions])
    row_copy = jnp.concatenate([jnp.zeros((pos_dev,), jnp.int32), jnp.ones((pos_dev,), jnp.int32)])
    cos_tab, sin_tab = rotary_tables(row_pos)
    summed = [
        jnp.zeros((shard.shape[0] * all_devices,) + shard.shape[1:], jnp.float32)
        for shard in shard_list
    ]
    outputs = []
    grad_inputs = []
    for micro_step in range(micro_count):
        gathered = (
            lax.all_gather(shard_list[0], ("batch", "ctx"), axis=0, tiled=True),
            lax.all_gather(shard_list[1], ("batch", "ctx"), axis=0, tiled=True),
            lax.all_gather(shard_list[2], ("batch", "ctx"), axis=0, tiled=True),
            lax.all_gather(shard_list[3], ("batch", "ctx"), axis=0, tiled=True),
            lax.all_gather(shard_list[4], ("batch", "ctx"), axis=0, tiled=True),
            lax.all_gather(shard_list[5], ("batch", "ctx"), axis=0, tiled=True),
            lax.all_gather(shard_list[6], ("batch", "ctx"), axis=0, tiled=True),
            lax.all_gather(shard_list[7], ("batch", "ctx"), axis=0, tiled=True),
            lax.all_gather(shard_list[8], ("batch", "ctx"), axis=0, tiled=True),
            lax.all_gather(shard_list[9], ("batch", "ctx"), axis=0, tiled=True),
            lax.all_gather(shard_list[10], ("batch", "ctx"), axis=0, tiled=True),
            lax.all_gather(shard_list[11], ("batch", "ctx"), axis=0, tiled=True),
        )
        prefix_len = prefix[micro_step]
        block_len = block_size[micro_step]
        inputs = layer_input[micro_step].reshape(row_count, width).astype(jnp.float32)
        normed = layer_norm(
            inputs, gathered[0].astype(jnp.float32), gathered[1].astype(jnp.float32)
        ).astype(jnp.bfloat16)
        projected = jnp.dot(normed, gathered[2], preferred_element_type=jnp.float32) + gathered[
            3
        ].astype(jnp.float32)
        query_rows = rotate(
            projected[:, :width].reshape(row_count, HEADS, HEAD_DIM), cos_tab, sin_tab
        ).astype(jnp.bfloat16)
        key_rows = rotate(
            projected[:, width : 2 * width].reshape(row_count, HEADS, HEAD_DIM), cos_tab, sin_tab
        ).astype(jnp.bfloat16)
        value_rows = (
            projected[:, 2 * width :].reshape(row_count, HEADS, HEAD_DIM).astype(jnp.bfloat16)
        )
        noisy_allowed = (
            (row_copy == 0)[:, None]
            & ((row_pos // block_len)[:, None] == (positions // block_len)[None, :])
        )[:, None, :]
        start_state = (
            jnp.full((row_count, HEADS), NEGATIVE, jnp.float32),
            jnp.zeros((row_count, HEADS), jnp.float32),
            jnp.zeros((row_count, HEADS, HEAD_DIM), jnp.float32),
        )
        state = absorb(
            start_state, query_rows, key_rows[:pos_dev], value_rows[:pos_dev], noisy_allowed
        )
        clean_kv = jnp.stack([key_rows[pos_dev:], value_rows[pos_dev:]]).reshape(2, pos_dev, width)
        running = state
        shard_piece = lax.all_gather(clean_kv, "ctx", axis=1, tiled=True)
        first_row = jnp.int32(0)
        piece_rows = shard_piece.shape[1]
        length = block_length(piece_rows)

        def inner(inner_state, block_index):
            block_kv = take_rows(shard_piece, block_index, length).reshape(
                2, length, HEADS, HEAD_DIM
            )
            key_pos = first_row + block_index * length + jnp.arange(length, dtype=jnp.int32)
            allowed = clean_allowed(row_copy, row_pos, key_pos, prefix_len, block_len)[:, None, :]
            result = lax.cond(
                jnp.any(allowed),
                lambda given: absorb(given, query_rows, block_kv[0], block_kv[1], allowed),
                lambda given: given,
                inner_state,
            )
            return (result, None)

        running, _ = lax.scan(inner, running, jnp.arange(piece_rows // length, dtype=jnp.int32))
        row_best, row_total, weighted = running
        attn = weighted / row_total[..., None]
        log_total = row_best + jnp.log(row_total)
        attn_low = attn.reshape(row_count, width).astype(jnp.bfloat16)
        hidden = (
            inputs
            + jnp.dot(attn_low, gathered[4], preferred_element_type=jnp.float32)
            + gathered[5].astype(jnp.float32)
        )
        normed_two = layer_norm(
            hidden, gathered[6].astype(jnp.float32), gathered[7].astype(jnp.float32)
        ).astype(jnp.bfloat16)
        upper = jnp.dot(normed_two, gathered[8], preferred_element_type=jnp.float32) + gathered[
            9
        ].astype(jnp.float32)
        activ = jax.nn.gelu(upper, approximate=True).astype(jnp.bfloat16)
        output = (
            hidden
            + jnp.dot(activ, gathered[10], preferred_element_type=jnp.float32)
            + gathered[11].astype(jnp.float32)
        )
        outputs.append(output.astype(jnp.bfloat16).reshape(2, pos_dev, width))
        back_full = (
            lax.all_gather(shard_list[0], ("batch", "ctx"), axis=0, tiled=True),
            lax.all_gather(shard_list[1], ("batch", "ctx"), axis=0, tiled=True),
            lax.all_gather(shard_list[2], ("batch", "ctx"), axis=0, tiled=True),
            lax.all_gather(shard_list[3], ("batch", "ctx"), axis=0, tiled=True),
            lax.all_gather(shard_list[4], ("batch", "ctx"), axis=0, tiled=True),
            lax.all_gather(shard_list[5], ("batch", "ctx"), axis=0, tiled=True),
            lax.all_gather(shard_list[6], ("batch", "ctx"), axis=0, tiled=True),
            lax.all_gather(shard_list[7], ("batch", "ctx"), axis=0, tiled=True),
            lax.all_gather(shard_list[8], ("batch", "ctx"), axis=0, tiled=True),
            lax.all_gather(shard_list[9], ("batch", "ctx"), axis=0, tiled=True),
            lax.all_gather(shard_list[10], ("batch", "ctx"), axis=0, tiled=True),
            lax.all_gather(shard_list[11], ("batch", "ctx"), axis=0, tiled=True),
        )
        grad_top = cotangent[micro_step].reshape(row_count, width).astype(jnp.float32)
        grad_top_low = grad_top.astype(jnp.bfloat16)
        summed[10] = summed[10] + jnp.einsum(
            "rf,rd->fd", activ, grad_top_low, preferred_element_type=jnp.float32
        )
        summed[11] = summed[11] + jnp.sum(grad_top, 0)
        grad_activ = jnp.einsum(
            "rd,fd->rf", grad_top_low, back_full[10], preferred_element_type=jnp.float32
        )
        _, gelu_back = jax.vjp(lambda pre_act: jax.nn.gelu(pre_act, approximate=True), upper)
        grad_upper = gelu_back(grad_activ)[0]
        grad_upper_low = grad_upper.astype(jnp.bfloat16)
        summed[8] = summed[8] + jnp.einsum(
            "rd,rf->df", normed_two, grad_upper_low, preferred_element_type=jnp.float32
        )
        summed[9] = summed[9] + jnp.sum(grad_upper, 0)
        grad_normed_two = jnp.einsum(
            "rf,df->rd", grad_upper_low, back_full[8], preferred_element_type=jnp.float32
        )
        _, norm_back_two = jax.vjp(
            layer_norm, hidden, back_full[6].astype(jnp.float32), back_full[7].astype(jnp.float32)
        )
        grad_hid_norm, grad_gain_two, grad_bias_two = norm_back_two(grad_normed_two)
        summed[6] = summed[6] + grad_gain_two
        summed[7] = summed[7] + grad_bias_two
        grad_hidden = grad_top + grad_hid_norm
        grad_hidden_low = grad_hidden.astype(jnp.bfloat16)
        summed[4] = summed[4] + jnp.einsum(
            "rd,re->de", attn_low, grad_hidden_low, preferred_element_type=jnp.float32
        )
        summed[5] = summed[5] + jnp.sum(grad_hidden, 0)
        grad_attn = jnp.einsum(
            "re,de->rd", grad_hidden_low, back_full[4], preferred_element_type=jnp.float32
        )
        grad_attn = grad_attn.reshape(row_count, HEADS, HEAD_DIM).astype(jnp.bfloat16)
        row_delta = jnp.sum(grad_attn.astype(jnp.float32) * attn, -1)
        probs_noisy, scores_noisy = score_grads(
            query_rows,
            grad_attn,
            log_total,
            row_delta,
            key_rows[:pos_dev],
            value_rows[:pos_dev],
            noisy_allowed,
        )
        grad_query = jnp.einsum(
            "rhk,khd->rhd", scores_noisy, key_rows[:pos_dev], preferred_element_type=jnp.float32
        )
        grad_key_noisy = jnp.einsum(
            "rhk,rhd->khd", scores_noisy, query_rows, preferred_element_type=jnp.float32
        )
        grad_value_noisy = jnp.einsum(
            "rhk,rhd->khd", probs_noisy, grad_attn, preferred_element_type=jnp.float32
        )
        my_keys = key_rows[pos_dev:]
        my_values = value_rows[pos_dev:]
        zero_rows = jnp.zeros((pos_dev, HEADS, HEAD_DIM), jnp.float32)
        query_pack = jnp.concatenate(
            [query_rows.reshape(2, pos_dev, width), grad_attn.reshape(2, pos_dev, width)], 0
        )
        log_pack = log_total.reshape(2, pos_dev, HEADS)
        delta_pack = row_delta.reshape(2, pos_dev, HEADS)

        def query_side(grad_now, block_keys, block_values, key_pos):
            allowed = clean_allowed(row_copy, row_pos, key_pos, prefix_len, block_len)[:, None, :]

            def query_compute(given):
                _, grad_score = score_grads(
                    query_rows, grad_attn, log_total, row_delta, block_keys, block_values, allowed
                )
                return given + jnp.einsum(
                    "rhk,khd->rhd", grad_score, block_keys, preferred_element_type=jnp.float32
                )

            return lax.cond(jnp.any(allowed), query_compute, lambda given: given, grad_now)

        def key_side(pair_now, block_pack, block_log, block_delta, query_pos):
            length = query_pos.shape[0]
            flat_query = block_pack[0:2].reshape(2 * length, HEADS, HEAD_DIM)
            flat_grad = block_pack[2:4].reshape(2 * length, HEADS, HEAD_DIM)
            flat_log = block_log.reshape(2 * length, HEADS)
            flat_delta = block_delta.reshape(2 * length, HEADS)
            query_copy = jnp.concatenate(
                [jnp.zeros((length,), jnp.int32), jnp.ones((length,), jnp.int32)]
            )
            both_pos = jnp.concatenate([query_pos, query_pos])
            allowed = clean_allowed(query_copy, both_pos, positions, prefix_len, block_len)[
                :, None, :
            ]

            def key_compute(given):
                prob_low, grad_score = score_grads(
                    flat_query, flat_grad, flat_log, flat_delta, my_keys, my_values, allowed
                )
                grad_keys_new = given[0] + jnp.einsum(
                    "rhk,rhd->khd", grad_score, flat_query, preferred_element_type=jnp.float32
                )
                grad_values_new = given[1] + jnp.einsum(
                    "rhk,rhd->khd", prob_low, flat_grad, preferred_element_type=jnp.float32
                )
                return (grad_keys_new, grad_values_new)

            return lax.cond(jnp.any(allowed), key_compute, lambda given: given, pair_now)

        def fold_keys_back(grad_now, shard_piece, first_row):
            piece_rows = shard_piece.shape[1]
            length = block_length(piece_rows)

            def inner(inner_grad, block_index):
                block_kv = take_rows(shard_piece, block_index, length).reshape(
                    2, length, HEADS, HEAD_DIM
                )
                key_pos = first_row + block_index * length + jnp.arange(length, dtype=jnp.int32)
                return (query_side(inner_grad, block_kv[0], block_kv[1], key_pos), None)

            grad_now, _ = lax.scan(
                inner, grad_now, jnp.arange(piece_rows // length, dtype=jnp.int32)
            )
            return grad_now

        grad_query = fold_keys_back(
            grad_query, lax.all_gather(clean_kv, "ctx", axis=1, tiled=True), jnp.int32(0)
        )

        def fold_queries_back(pair_now, shard_pieces, first_row):
            pack_piece, log_piece, delta_piece = shard_pieces
            piece_rows = pack_piece.shape[1]
            length = block_length(piece_rows)

            def inner(inner_pair, block_index):
                block_pack = take_rows(pack_piece, block_index, length).reshape(
                    4, length, HEADS, HEAD_DIM
                )
                block_log = take_rows(log_piece, block_index, length)
                block_delta = take_rows(delta_piece, block_index, length)
                query_pos = first_row + block_index * length + jnp.arange(length, dtype=jnp.int32)
                return (key_side(inner_pair, block_pack, block_log, block_delta, query_pos), None)

            pair_now, _ = lax.scan(
                inner, pair_now, jnp.arange(piece_rows // length, dtype=jnp.int32)
            )
            return pair_now

        grad_key_clean, grad_value_clean = fold_queries_back(
            (zero_rows, zero_rows),
            (
                lax.all_gather(query_pack.astype(jnp.float32), "ctx", axis=1, tiled=True).astype(
                    jnp.bfloat16
                ),
                lax.all_gather(log_pack, "ctx", axis=1, tiled=True),
                lax.all_gather(delta_pack, "ctx", axis=1, tiled=True),
            ),
            jnp.int32(0),
        )
        grad_keys = jnp.concatenate([grad_key_noisy, grad_key_clean], 0)
        grad_values = jnp.concatenate([grad_value_noisy, grad_value_clean], 0)
        _, rotate_back = jax.vjp(lambda turned: rotate(turned, cos_tab, sin_tab), grad_query)
        grad_query_pre = rotate_back(grad_query)[0]
        grad_key_pre = rotate_back(grad_keys)[0]
        grad_projected = jnp.concatenate(
            [
                grad_query_pre.reshape(row_count, width),
                grad_key_pre.reshape(row_count, width),
                grad_values.reshape(row_count, width),
            ],
            -1,
        )
        grad_projected_low = grad_projected.astype(jnp.bfloat16)
        summed[2] = summed[2] + jnp.einsum(
            "rd,rf->df", normed, grad_projected_low, preferred_element_type=jnp.float32
        )
        summed[3] = summed[3] + jnp.sum(grad_projected, 0)
        grad_normed = jnp.einsum(
            "rf,df->rd", grad_projected_low, back_full[2], preferred_element_type=jnp.float32
        )
        _, norm_back_one = jax.vjp(
            layer_norm, inputs, back_full[0].astype(jnp.float32), back_full[1].astype(jnp.float32)
        )
        grad_in_norm, grad_gain_one, grad_bias_one = norm_back_one(grad_normed)
        summed[0] = summed[0] + grad_gain_one
        summed[1] = summed[1] + grad_bias_one
        grad_inputs.append(
            (grad_hidden + grad_in_norm).astype(jnp.bfloat16).reshape(2, pos_dev, width)
        )
    reduced = (
        lax.psum_scatter(summed[0], ("batch", "ctx"), scatter_dimension=0, tiled=True),
        lax.psum_scatter(summed[1], ("batch", "ctx"), scatter_dimension=0, tiled=True),
        lax.psum_scatter(summed[2], ("batch", "ctx"), scatter_dimension=0, tiled=True),
        lax.psum_scatter(summed[3][: 2 * width], ("batch", "ctx"), scatter_dimension=0, tiled=True),
        lax.psum_scatter(summed[3][2 * width :], ("batch", "ctx"), scatter_dimension=0, tiled=True),
        lax.psum_scatter(summed[4], ("batch", "ctx"), scatter_dimension=0, tiled=True),
        lax.psum_scatter(summed[5], ("batch", "ctx"), scatter_dimension=0, tiled=True),
        lax.psum_scatter(summed[6], ("batch", "ctx"), scatter_dimension=0, tiled=True),
        lax.psum_scatter(summed[7], ("batch", "ctx"), scatter_dimension=0, tiled=True),
        lax.psum_scatter(summed[8], ("batch", "ctx"), scatter_dimension=0, tiled=True),
        lax.psum_scatter(summed[9], ("batch", "ctx"), scatter_dimension=0, tiled=True),
        lax.psum_scatter(summed[10], ("batch", "ctx"), scatter_dimension=0, tiled=True),
        lax.psum_scatter(summed[11], ("batch", "ctx"), scatter_dimension=0, tiled=True),
    )
    return (jnp.stack(outputs), jnp.stack(grad_inputs)) + tuple(reduced)


def solution(mesh):
    return jax.shard_map(
        on_device,
        mesh=mesh,
        in_specs=(
            P("batch", None, "ctx", None),
            P("batch", None, "ctx", None),
            P("batch"),
            P("batch"),
            P(("batch", "ctx")),
            P(("batch", "ctx")),
            P(("batch", "ctx"), None),
            P(("batch", "ctx")),
            P(("batch", "ctx"), None),
            P(("batch", "ctx")),
            P(("batch", "ctx")),
            P(("batch", "ctx")),
            P(("batch", "ctx"), None),
            P(("batch", "ctx")),
            P(("batch", "ctx"), None),
            P(("batch", "ctx")),
        ),
        out_specs=(
            P("batch", None, "ctx", None),
            P("batch", None, "ctx", None),
            P(("batch", "ctx")),
            P(("batch", "ctx")),
            P(("batch", "ctx"), None),
            P(("batch", "ctx")),
            P(("batch", "ctx")),
            P(("batch", "ctx"), None),
            P(("batch", "ctx")),
            P(("batch", "ctx")),
            P(("batch", "ctx")),
            P(("batch", "ctx"), None),
            P(("batch", "ctx")),
            P(("batch", "ctx"), None),
            P(("batch", "ctx")),
        ),
        check_vma=False,
    )
```

profile of v0, /device:TPU:0, one launch (start us, length us, event | category | flops | bytes accessed | tf_op | source)
XLA Modules:
  0.0 1300.4 jit_solution(14263877350277734049)
XLA Ops:
  15.5 42.8 %all-reduce.26 = (bf16[2304]{0:T(1024)(128)(2,1)S(1)}, bf16[768]{0:T(1024)(128)(2,1)S(1)}, bf16[768]{0:T(1024)(128)(2,1)S(1)}, bf16[768]{0:T(1024)(128)(2,1)S(1)...) all-reduce(bf16[2304]{0:T(1024)(128)(2,1)S(1)} %dynamic-update-slic, ...), channel_id=1, replica_groups=mesh['batch'=2,'ctx'=16] {'batch','ctx'}, use_global_device_ids=true, to_apply=%add.10 | all-reduce | flops 9984 | bytes 39936
  101.3 37.8 %all-gather.17.cloned.1.call-done = bf16[3072,768]{1,0:T(8,128)(2,1)} async-done(((bf16[96,768]{1,0:T(8,128)(2,1)}), bf16[3072,768]{1,0:T(8,128)(2,1)}) %all-gather.17.cloned.1.call-update) | async-done | bytes 4718608 | tf_op jit(solution)/shard_map/all_gather | solution.py:150
  144.5 49.7 %all-gather.11.cloned.1.call-done = bf16[2,1536,768]{2,1,0:T(8,128)(2,1)} async-done(((bf16[2,96,768]{2,1,0:T(8,128)(2,1)}), bf16[2,1536,768]{2,1,0:T(8,128)(2,1)}) %all-gather.11.cloned.1.call-update) | async-done | bytes 4718608 | tf_op jit(solution)/shard_map/all_gather | solution.py:185
  200.9 21.6 %while.100 = (s32[]{:T(128)}, f32[192,12]{0,1:T(8,128)S(1)}, f32[192,12]{0,1:T(8,128)S(1)}, f32[192,12,64]{0,2,1:T(8,128)S(1)}, s32[2]{0:T(128)S(1)}, /*index=5*...) while((s32[]{:T(128)}, f32[192,12]{0,1:T(8,128)S(1)}, ...), condition=%wide.region_10.11_spmd, body=%wide.region_4.10_spmd.sunk | while | flops 477477312 | bytes 30536632 | solution.py:204
  223.4 26.2 %all-gather.13.cloned.1.call-done = bf16[768,768]{1,0:T(8,128)(2,1)} async-done(((bf16[24,768]{1,0:T(8,128)(2,1)}), bf16[768,768]{1,0:T(8,128)(2,1)}) %all-gather.13.cloned.1.call-update) | async-done | bytes 1179664 | tf_op jit(solution)/shard_map/all_gather | solution.py:144
  251.9 62.9 %all-gather.15.cloned.1.call-done = bf16[768,3072]{1,0:T(8,128)(2,1)} async-done(((bf16[24,3072]{1,0:T(8,128)(2,1)}), bf16[768,3072]{1,0:T(8,128)(2,1)}) %all-gather.15.cloned.1.call-update) | async-done | bytes 4718608 | tf_op jit(solution)/shard_map/all_gather | solution.py:148
  336.3 34.2 %all_gather.101 = f32[2,1536,12]{2,0,1:T(2,128)} all-gather(f32[2,96,12]{2,0,1:T(2,128)S(1)} %copy.191), channel_id=1, replica_groups=mesh['batch'=2,'ctx'=16] {'ctx'}, dimensions={1}, use_global_device_ids=true | all-gather | bytes 156672 | tf_op jit(solution)/shard_map/all_gather | solution.py:390
  376.5 35.2 %all_gather.102 = f32[2,1536,12]{2,0,1:T(2,128)} all-gather(f32[2,96,12]{2,0,1:T(2,128)S(1)} %copy.193), channel_id=1, replica_groups=mesh['batch'=2,'ctx'=16] {'ctx'}, dimensions={1}, use_global_device_ids=true | all-gather | bytes 156672 | tf_op jit(solution)/shard_map/all_gather | solution.py:391
  418.1 27.8 %while.102 = (s32[]{:T(128)}, f32[192,12,64]{0,2,1:T(8,128)}, s32[2]{0:T(128)S(1)}, s32[]{:T(128)}, s32[]{:T(128)}, /*index=5*/s32[192,1]{0,1:T(1,128)S(1)}, s32...) while((s32[]{:T(128)}, f32[192,12,64]{0,2,1:T(8,128)}, ...), condition=%wide.region_33.34_spmd, body=%wide.region_29.33_spmd.sunk | while | flops 694970304 | bytes 24509336 | solution.py:356
  424.5 14.9 %conditional.18 = (f32[192,12,64]{0,2,1:T(8,128)}) conditional(s32[]{:T(128)} %convert_element_type.527, f32[192,12,64]{0,2,1:T(8,128)} %get-tuple-element.3163, (pred[192,1,768]{2,0,1:T(8,128)(4,1)S(1)}, s32[]{:T(128)}, bf16[2,1536,768]{1,2,0:T(8,128)(2,1)}, bf16[192,12,64]{0,2,1:T(8,128)(2,1)S(1)}, f32[192,12]{0,1:T(8,128)}, ...), branch_computations={%region_31.31_spmd, %region_32.32_spmd} | conditional | flops 693780480 | bytes 24348734 | solution.py:315
  446.0 19.4 %copy.194 = bf16[4,1536,768]{1,0,2:T(4,128)(2,1)} copy(bf16[4,1536,768]{2,0,1:T(4,128)(2,1)} %all-gather.21.cloned.1.call-done) | data formatting | bytes 18874368
  467.0 100.9 %while.104 = (s32[]{:T(128)}, f32[96,12,64]{0,2,1:T(8,128)}, f32[96,12,64]{0,2,1:T(8,128)}, s32[]{:T(128)}, s32[]{:T(128)}, /*index=5*/s32[2]{0:T(128)S(1)}, s32...) while((s32[]{:T(128)}, f32[96,12,64]{0,2,1:T(8,128)}, ...), condition=%wide.region_38.39_spmd.clone.clone, body=%wide.region_34.38_spmd.clone.clone.sunk | while | flops 930320256 | bytes 62183272 | solution.py:379
  472.9 44.8 %conditional.20 = ((f32[96,12,64]{0,2,1:T(8,128)}, f32[96,12,64]{0,2,1:T(8,128)})) conditional(s32[]{:T(128)} %convert_element_type.529, (f32[96,12,64]{0,2,1:T(8,128)}, f32[96,12,64]{0,2,1:T(8,128)}) %tuple.426, (pred[1536,1,96]{0,2,1:T(8,128)(4,1)S(1)}, s32[]{:T(128)}, bf16[4,1536,768]{1,0,2:T(4,128)(2,1)}, bf16[96,12,64]{0,2,1:T(8,128)(2,1)S(1)}, ...), branch_computations={%region_36.36_spmd, %region_37.37_spmd} | conditional | flops 929120256 | bytes 62005364 | solution.py:343
  472.9 14.3 %constant_dynamic-slice_fusion.7 = (bf16[2,768,768]{1,0,2:T(2,128)(2,1)S(1)}, bf16[2,768,768]{1,0,2:T(2,128)(2,1)}) fusion(bf16[4,1536,768]{1,0,2:T(4,128)(2,1)} %get-tuple-element.1618, s32[]{:T(128)S(6)} %add.920, s32[]{:T(128)S(6)} %select_n.367), kind=kLoop, calls=%fused_computation.73 | loop fusion | bytes 9437192 | tf_op jit(solution)/shard_map/while/body/eval_jaxpr/slice | solution.py:320
  523.4 44.1 %conditional.20 = ((f32[96,12,64]{0,2,1:T(8,128)}, f32[96,12,64]{0,2,1:T(8,128)})) conditional(s32[]{:T(128)} %convert_element_type.529, (f32[96,12,64]{0,2,1:T(8,128)}, f32[96,12,64]{0,2,1:T(8,128)}) %tuple.426, (pred[1536,1,96]{0,2,1:T(8,128)(4,1)S(1)}, s32[]{:T(128)}, bf16[4,1536,768]{1,0,2:T(4,128)(2,1)}, bf16[96,12,64]{0,2,1:T(8,128)(2,1)S(1)}, ...), branch_computations={%region_36.36_spmd, %region_37.37_spmd} | conditional | flops 929120256 | bytes 62005364 | solution.py:343
  523.4 13.7 %constant_dynamic-slice_fusion.7 = (bf16[2,768,768]{1,0,2:T(2,128)(2,1)S(1)}, bf16[2,768,768]{1,0,2:T(2,128)(2,1)}) fusion(bf16[4,1536,768]{1,0,2:T(4,128)(2,1)} %get-tuple-element.1618, s32[]{:T(128)S(6)} %add.920, s32[]{:T(128)S(6)} %select_n.367), kind=kLoop, calls=%fused_computation.73 | loop fusion | bytes 9437192 | tf_op jit(solution)/shard_map/while/body/eval_jaxpr/slice | solution.py:320
  580.5 47.0 %all-gather.19.cloned.1.call-done = bf16[2,1536,768]{2,1,0:T(8,128)(2,1)} async-done(((bf16[2,96,768]{2,1,0:T(8,128)(2,1)}), bf16[2,1536,768]{2,1,0:T(8,128)(2,1)}) %all-gather.19.cloned.1.call-update) | async-done | bytes 4718608 | tf_op jit(solution)/shard_map/all_gather | solution.py:185
  634.1 21.9 %while.101 = (s32[]{:T(128)}, f32[192,12]{0,1:T(8,128)S(1)}, f32[192,12]{0,1:T(8,128)S(1)}, f32[192,12,64]{0,2,1:T(8,128)S(1)}, s32[2]{0:T(128)S(1)}, /*index=5*...) while((s32[]{:T(128)}, f32[192,12]{0,1:T(8,128)S(1)}, ...), condition=%wide.region_23.24_spmd, body=%wide.region_17.23_spmd.sunk | while | flops 477477312 | bytes 30536632 | solution.py:204
  709.3 43.8 %all_gather.104 = f32[2,1536,12]{2,0,1:T(2,128)} all-gather(f32[2,96,12]{2,0,1:T(2,128)S(1)} %copy.204), channel_id=1, replica_groups=mesh['batch'=2,'ctx'=16] {'ctx'}, dimensions={1}, use_global_device_ids=true | all-gather | bytes 156672 | tf_op jit(solution)/shard_map/all_gather | solution.py:390
  756.6 32.8 %all_gather.105 = f32[2,1536,12]{2,0,1:T(2,128)} all-gather(f32[2,96,12]{2,0,1:T(2,128)S(1)} %copy.206), channel_id=1, replica_groups=mesh['batch'=2,'ctx'=16] {'ctx'}, dimensions={1}, use_global_device_ids=true | all-gather | bytes 156672 | tf_op jit(solution)/shard_map/all_gather | solution.py:391
  797.9 27.6 %while.103 = (s32[]{:T(128)}, f32[192,12,64]{0,2,1:T(8,128)}, s32[2]{0:T(128)S(1)}, s32[]{:T(128)}, s32[]{:T(128)}, /*index=5*/s32[192,1]{0,1:T(1,128)S(1)}, s32...) while((s32[]{:T(128)}, f32[192,12,64]{0,2,1:T(8,128)}, ...), condition=%wide.region_48.49_spmd, body=%wide.region_44.48_spmd.sunk | while | flops 694970304 | bytes 24546228 | solution.py:356
  804.3 14.8 %conditional.19 = (f32[192,12,64]{0,2,1:T(8,128)}) conditional(s32[]{:T(128)} %convert_element_type.528, f32[192,12,64]{0,2,1:T(8,128)} %get-tuple-element.3352, (pred[192,1,768]{2,0,1:T(8,128)(4,1)S(1)}, s32[]{:T(128)}, bf16[2,1536,768]{1,2,0:T(8,128)(2,1)}, bf16[192,12,64]{0,2,1:T(8,128)(2,1)S(1)}, f32[192,12]{0,1:T(8,128)}, ...), branch_computations={%region_46.46_spmd, %region_47.47_spmd} | conditional | flops 693780480 | bytes 24385626 | solution.py:315
  825.5 19.4 %copy.207 = bf16[4,1536,768]{1,0,2:T(4,128)(2,1)} copy(bf16[4,1536,768]{2,0,1:T(4,128)(2,1)} %all-gather.23.cloned.1.call-done) | data formatting | bytes 18874368
  846.5 101.4 %while.105 = (s32[]{:T(128)}, f32[96,12,64]{0,2,1:T(8,128)}, f32[96,12,64]{0,2,1:T(8,128)}, s32[]{:T(128)}, s32[]{:T(128)}, /*index=5*/s32[2]{0:T(128)S(1)}, s32...) while((s32[]{:T(128)}, f32[96,12,64]{0,2,1:T(8,128)}, ...), condition=%wide.region_53.54_spmd.clone.clone, body=%wide.region_49.53_spmd.clone.clone.sunk | while | flops 930320256 | bytes 62183272 | solution.py:379
  852.4 44.4 %conditional.21 = ((f32[96,12,64]{0,2,1:T(8,128)}, f32[96,12,64]{0,2,1:T(8,128)})) conditional(s32[]{:T(128)} %convert_element_type.530, (f32[96,12,64]{0,2,1:T(8,128)}, f32[96,12,64]{0,2,1:T(8,128)}) %tuple.431, (pred[1536,1,96]{0,2,1:T(8,128)(4,1)S(1)}, s32[]{:T(128)}, bf16[4,1536,768]{1,0,2:T(4,128)(2,1)}, bf16[96,12,64]{0,2,1:T(8,128)(2,1)S(1)}, ...), branch_computations={%region_51.51_spmd, %region_52.52_spmd} | conditional | flops 929120256 | bytes 62005364 | solution.py:343
  852.4 13.8 %constant_dynamic-slice_fusion.11 = (bf16[2,768,768]{1,0,2:T(2,128)(2,1)S(1)}, bf16[2,768,768]{1,0,2:T(2,128)(2,1)}) fusion(bf16[4,1536,768]{1,0,2:T(4,128)(2,1)} %get-tuple-element.1666, s32[]{:T(128)S(6)} %add.922, s32[]{:T(128)S(6)} %select_n.380), kind=kLoop, calls=%fused_computation.117 | loop fusion | bytes 9437192 | tf_op jit(solution)/shard_map/while/body/eval_jaxpr/slice | solution.py:320
  902.5 45.2 %conditional.21 = ((f32[96,12,64]{0,2,1:T(8,128)}, f32[96,12,64]{0,2,1:T(8,128)})) conditional(s32[]{:T(128)} %convert_element_type.530, (f32[96,12,64]{0,2,1:T(8,128)}, f32[96,12,64]{0,2,1:T(8,128)}) %tuple.431, (pred[1536,1,96]{0,2,1:T(8,128)(4,1)S(1)}, s32[]{:T(128)}, bf16[4,1536,768]{1,0,2:T(4,128)(2,1)}, bf16[96,12,64]{0,2,1:T(8,128)(2,1)S(1)}, ...), branch_computations={%region_51.51_spmd, %region_52.52_spmd} | conditional | flops 929120256 | bytes 62005364 | solution.py:343
  902.6 13.7 %constant_dynamic-slice_fusion.11 = (bf16[2,768,768]{1,0,2:T(2,128)(2,1)S(1)}, bf16[2,768,768]{1,0,2:T(2,128)(2,1)}) fusion(bf16[4,1536,768]{1,0,2:T(4,128)(2,1)} %get-tuple-element.1666, s32[]{:T(128)S(6)} %add.922, s32[]{:T(128)S(6)} %select_n.380), kind=kLoop, calls=%fused_computation.117 | loop fusion | bytes 9437192 | tf_op jit(solution)/shard_map/while/body/eval_jaxpr/slice | solution.py:320
  931.5 9.4 fusion.121
  974.4 39.9 %all-reduce.25 = (f32[768]{0:T(1024)S(1)}, f32[768]{0:T(1024)S(1)}, f32[1536]{0:T(1024)S(1)}, f32[768]{0:T(1024)S(1)}, f32[768]{0:T(1024)S(1)}, /*index=5*/f32[7...) all-reduce(f32[768]{0:T(1024)S(1)} %add.811, ...), channel_id=2, replica_groups=mesh['batch'=2,'ctx'=16] {'batch','ctx'}, use_global_device_ids=true, to_apply=%region_58.59.clone | all-reduce | flops 9984 | bytes 79872
  1026.7 141.3 %reduce-scatter.11.cloned.1.call-done = f32[96,768]{1,0:T(8,128)} async-done(((f32[3072,768]{1,0:T(8,128)}), f32[96,768]{1,0:T(8,128)}) %reduce-scatter.11.cloned.1.call-update) | async-done | bytes 294928 | tf_op jit(solution)/shard_map/reduce_scatter | solution.py:437
  1168.0 125.2 %reduce-scatter.5.cloned.1.call-done = f32[24,2304]{1,0:T(8,128)} async-done(((f32[768,2304]{1,0:T(8,128)}), f32[24,2304]{1,0:T(8,128)}) %reduce-scatter.5.cloned.1.call-update) | async-done | bytes 221200 | tf_op jit(solution)/shard_map/reduce_scatter | solution.py:428
  (707 shorter events, 460.0 us)
Async XLA Ops:
  7.2 66.7 %all-gather.9.cloned.1.call-start = ((), (), s32[]{:S(2)}) async-start(), calls=%async_computation.4 | async-start | bytes 3649536 | tf_op jit(solution)/shard_map/all_gather | solution.py:142
  7.9 131.2 %all-gather.17.cloned.1.call-start = ((), (), s32[]{:S(2)}) async-start(), calls=%async_computation.8 | async-start | bytes 4866048 | tf_op jit(solution)/shard_map/all_gather | solution.py:150
  8.7 185.5 %all-gather.11.cloned.1.call-start = ((), (), s32[]{:S(2)}) async-start(), calls=%async_computation.5 | async-start | bytes 5013504 | tf_op jit(solution)/shard_map/all_gather | solution.py:185
  81.8 167.9 %all-gather.13.cloned.1.call-start = ((), (), s32[]{:S(2)}) async-start(), calls=%async_computation.6 | async-start | bytes 1216512 | tf_op jit(solution)/shard_map/all_gather | solution.py:144
  82.3 232.5 %all-gather.15.cloned.1.call-start = ((), (), s32[]{:S(2)}) async-start(), calls=%async_computation.7 | async-start | bytes 4866048 | tf_op jit(solution)/shard_map/all_gather | solution.py:148
  82.9 363.1 %all-gather.21.cloned.1.call-start = ((), (), s32[]{:S(2)}) async-start(), calls=%async_computation.10 | async-start | bytes 10027008 | tf_op jit(solution)/shard_map/all_gather | solution.py:387
  83.7 241.9 %copy-start.97 = (f32[768]{0:T(1024)}, f32[768]{0:T(1024)S(1)}, u32[]{:S(2)}) copy-start(f32[768]{0:T(1024)S(1)} %convert_element_type.316) | copy-start | bytes 9220
  84.3 230.6 %copy-start.103 = (f32[768]{0:T(1024)}, f32[768]{0:T(1024)S(1)}, u32[]{:S(2)}) copy-start(f32[768]{0:T(1024)S(1)} %convert_element_type.317) | copy-start | bytes 9220
  89.6 236.4 %copy-start.37 = (bf16[1,2,96,768]{3,2,1,0:T(8,128)(2,1)}, bf16[1,2,96,768]{3,2,1,0:T(8,128)(2,1)S(1)}, u32[]{:S(2)}) copy-start(bf16[1,2,96,768]{3,2,1,0:T(8,128)(2,1)S(1)} %get-tuple-element.2494) | copy-start | bytes 884740
  100.6 313.7 %copy-start.2 = (f32[192,12,96]{0,2,1:T(8,128)}, f32[192,12,96]{0,2,1:T(8,128)S(1)}, u32[]{:S(2)}) copy-start(f32[192,12,96]{0,2,1:T(8,128)S(1)} %get-tuple-element.2527) | copy-start | bytes 2654212
  200.9 48.7 %copy-start.118 = (f32[768]{0:T(1024)S(1)}, f32[768]{0:T(1024)}, u32[]{:S(2)}) copy-start(f32[768]{0:T(1024)} %convert_element_type.315) | copy-start | bytes 9220
  222.6 92.3 %copy-start.135 = (f32[3072]{0:T(1024)S(1)}, f32[3072]{0:T(1024)}, u32[]{:S(2)}) copy-start(f32[3072]{0:T(1024)} %convert_element_type.319) | copy-start | bytes 36868
  251.7 73.9 %copy-start.15 = (f32[192,768]{1,0:T(8,128)}, f32[192,768]{1,0:T(8,128)S(1)}, u32[]{:S(2)}) copy-start(f32[192,768]{1,0:T(8,128)S(1)} %get-tuple-element.2529) | copy-start | bytes 1769476
  251.7 73.9 %copy-start.120 = (f32[192]{0:T(256)}, f32[192]{0:T(256)S(1)}, u32[]{:S(2)}) copy-start(f32[192]{0:T(256)S(1)} %broadcast_multiply_fusion.1) | copy-start | bytes 2308
  251.9 73.7 %copy-start.129 = (f32[192]{0:T(256)}, f32[192]{0:T(256)S(1)}, u32[]{:S(2)}) copy-start(f32[192]{0:T(256)S(1)} %fusion.234) | copy-start | bytes 2308
  328.9 298.6 %all-gather.19.cloned.1.call-start = ((), (), s32[]{:S(2)}) async-start(), calls=%async_computation.9 | async-start | bytes 5013504 | tf_op jit(solution)/shard_map/all_gather | solution.py:185
  373.8 40.5 %copy-start.71 = (bf16[96,768]{0,1:T(8,128)(2,1)S(1)}, bf16[96,768]{0,1:T(8,128)(2,1)}, u32[]{:S(2)}) copy-start(bf16[96,768]{0,1:T(8,128)(2,1)} %copy.175) | copy-start | bytes 442372
  572.4 253.2 %all-gather.23.cloned.1.call-start = ((), (), s32[]{:S(2)}) async-start(), calls=%async_computation.11 | async-start | bytes 10027008 | tf_op jit(solution)/shard_map/all_gather | solution.py:387
  580.5 53.6 %copy-start.73 = (s32[192]{0:T(256)S(1)}, s32[192]{0:T(256)}, u32[]{:S(2)}) copy-start(s32[192]{0:T(256)} %copy-done.72) | copy-start | bytes 2308
  580.5 53.6 %copy-start.101 = (s32[192,1]{0,1:T(1,128)S(1)}, s32[192,1]{0,1:T(1,128)}, u32[]{:S(2)}) copy-start(s32[192,1]{0,1:T(1,128)} %copy-done.100) | copy-start | bytes 2308
  672.7 350.0 %reduce-scatter.7.cloned.1.call-start = ((), (), s32[]{:S(2)}) async-start(), calls=%async_computation.13 | async-start | bytes 2433024 | tf_op jit(solution)/shard_map/reduce_scatter | solution.py:431
  676.3 350.4 %reduce-scatter.9.cloned.1.call-start = ((), (), s32[]{:S(2)}) async-start(), calls=%async_computation.14 | async-start | bytes 9732096 | tf_op jit(solution)/shard_map/reduce_scatter | solution.py:435
  685.6 482.4 %reduce-scatter.11.cloned.1.call-start = ((), (), s32[]{:S(2)}) async-start(), calls=%async_computation.15 | async-start | bytes 9732096 | tf_op jit(solution)/shard_map/reduce_scatter | solution.py:437
  696.3 596.9 %reduce-scatter.5.cloned.1.call-start = ((), (), s32[]{:S(2)}) async-start(), calls=%async_computation.12 | async-start | bytes 7299072 | tf_op jit(solution)/shard_map/reduce_scatter | solution.py:428
  707.5 48.7 %copy-start.24 = (f32[192,12,64]{0,2,1:T(8,128)S(1)}, f32[192,12,64]{0,2,1:T(8,128)}, u32[]{:S(2)}) copy-start(f32[192,12,64]{0,2,1:T(8,128)} %copy-done.23) | copy-start | bytes 1769476
  756.2 36.3 %copy-start.69 = (bf16[96,768]{0,1:T(8,128)(2,1)S(1)}, bf16[96,768]{0,1:T(8,128)(2,1)}, u32[]{:S(2)}) copy-start(bf16[96,768]{0,1:T(8,128)(2,1)} %copy-done.68) | copy-start | bytes 442372
  756.2 36.3 %copy-start.85 = (pred[192,96]{0,1:T(8,128)(4,1)S(1)}, pred[192,96]{0,1:T(8,128)(4,1)}, u32[]{:S(2)}) copy-start(pred[192,96]{0,1:T(8,128)(4,1)} %get-tuple-element.2517) | copy-start | bytes 55300
  846.5 102.8 %copy-start.89 = (f32[192,32]{0,1:T(8,128)S(1)}, f32[192,32]{0,1:T(8,128)}, u32[]{:S(2)}) copy-start(f32[192,32]{0,1:T(8,128)} %copy-done.88) | copy-start | bytes 73732
  846.5 102.8 %copy-start.91 = (f32[192,32]{0,1:T(8,128)S(1)}, f32[192,32]{0,1:T(8,128)}, u32[]{:S(2)}) copy-start(f32[192,32]{0,1:T(8,128)} %copy-done.90) | copy-start | bytes 73732
  972.1 46.3 %copy-start.144 = (f32[192]{0:T(256)S(1)}, f32[192]{0:T(256)}, u32[]{:S(2)}) copy-start(f32[192]{0:T(256)} %copy-done.143) | copy-start | bytes 2308
  972.1 46.3 %copy-start.146 = (f32[192]{0:T(256)S(1)}, f32[192]{0:T(256)}, u32[]{:S(2)}) copy-start(f32[192]{0:T(256)} %copy-done.145) | copy-start | bytes 2308
  974.4 47.1 %copy-start.22 = (f32[192,768]{1,0:T(8,128)S(1)}, f32[192,768]{1,0:T(8,128)}, u32[]{:S(2)}) copy-start(f32[192,768]{1,0:T(8,128)} %copy-done.21) | copy-start | bytes 1769476
  (140 other events, 1043.0 us)
Sparse Core Ops, SparseCore 0:
  10.9 62.8 all-gather.8
  76.8 62.2 all-gather.16
  141.9 52.2 all-gather.10
  197.0 52.6 all-gather.12
  252.4 62.4 all-gather.14
  329.0 102.9 all-gather.20
  572.5 54.9 all-gather.18
  672.8 106.2 all-gather.22
  785.0 99.6 reduce-scatter.6
  892.1 134.6 reduce-scatter.8
  1033.2 134.7 reduce-scatter.10
  1175.1 118.0 reduce-scatter.4
where the time goes:
time: 1310 us; the launch traced here: 1300 us
  waiting for transfers between devices  504 us (38%)
  blocking collectives  229 us (17%)
  local copies, waits for them, and re-layouts  224 us (17%)
  matrix products  215 us (16%)
  other arithmetic  92.1 us (7%)
  between operations  18 us (1%)
  loops' own time  17.6 us (1%)
    reduce_scatter x1, waiting for transfers between devices, on_device(): lax.psum_scatter(summed[10], ('batch', 'ctx'), scatter_dimension=0, tiled...  141 us
    reduce_scatter x1, waiting for transfers between devices, on_device(): lax.psum_scatter(summed[2], ('batch', 'ctx'), scatter_dimension=0, tiled=...  125 us
    all_gather x2, waiting for transfers between devices, on_device(): shard_piece = lax.all_gather(clean_kv, 'ctx', axis=1, tiled=True)  96.7 us
    unnamed x2, blocking collectives  82.7 us
    all_gather x2, blocking collectives, on_device(): lax.all_gather(log_pack, 'ctx', axis=1, tiled=True)  78.1 us
    unnamed x341, local copies, waits for them, and re-layouts  71.4 us
    all_gather x2, blocking collectives, on_device(): lax.all_gather(delta_pack, 'ctx', axis=1, tiled=True)  68 us
    all_gather x1, waiting for transfers between devices, on_device(): lax.all_gather(shard_list[8], ('batch', 'ctx'), axis=0, tiled=True)  62.9 us
  transfers between devices with their start and end apart: 12, of which 9 were waited for; matrix products, arithmetic and copies ran while one was open for 27% of the time, Pallas kernels for 0%

commit v1 on v0

v1 whole, which is shorter than its diff:
```python
import functools

import jax
import jax.numpy as jnp
from jax import lax
from jax.experimental import pallas as pl
from jax.experimental.pallas import tpu as pltpu
from jax.sharding import PartitionSpec as P

HEADS = 12
HEAD_DIM = 64
SCALE = 0.125
NEGATIVE = -1e30
EPSILON = 1e-05
THETA = 10000.0
LANES = 128
BF16 = jnp.bfloat16
F32 = jnp.float32
VMEM_LIMIT = 56 * 1024 * 1024
NT = (((1,), (1,)), ((), ()))


def swap_halves(tile):
    lane = lax.broadcasted_iota(jnp.int32, tile.shape, 1)
    return jnp.where(lane % 64 < 32, pltpu.roll(tile, LANES - 32, 1), pltpu.roll(tile, 32, 1))


def project_kernel(x_ref, gain_ref, bias_ref, w_ref, add_ref, cos_ref, sin_ref, out_ref, unit_ref, *, start, turned):
    x = x_ref[...].astype(F32)
    center = x - jnp.mean(x, -1, keepdims=True)
    spread = jnp.mean(center * center, -1, keepdims=True)
    unit = center * lax.rsqrt(spread + EPSILON)
    unit_ref[...] = unit.astype(BF16)
    normed = (unit * gain_ref[...] + bias_ref[...]).astype(BF16)
    cos_tab, sin_tab = cos_ref[...], sin_ref[...]
    total = jnp.dot(normed, w_ref[:, start:], preferred_element_type=F32) + add_ref[:, start:]
    for tile in range(total.shape[1] // LANES):
        part = total[:, tile * LANES : (tile + 1) * LANES]
        if tile * LANES < turned:
            part = part * cos_tab + swap_halves(part) * sin_tab
        out_ref[:, tile * LANES : (tile + 1) * LANES] = part.astype(BF16)


def project(x, gain, bias, weight, add, cos_tab, sin_tab, start, turned, block):
    rows, width = x.shape
    columns = weight.shape[1] - start
    row_map = lambda i: (i, 0)
    fixed = lambda i: (0, 0)
    return pl.pallas_call(
        functools.partial(project_kernel, start=start, turned=turned),
        grid=(rows // block,),
        in_specs=[
            pl.BlockSpec((block, width), row_map),
            pl.BlockSpec((1, width), fixed),
            pl.BlockSpec((1, width), fixed),
            pl.BlockSpec(weight.shape, fixed),
            pl.BlockSpec((1, weight.shape[1]), fixed),
            pl.BlockSpec((block, LANES), row_map),
            pl.BlockSpec((block, LANES), row_map),
        ],
        out_specs=[pl.BlockSpec((block, columns), row_map), pl.BlockSpec((block, width), row_map)],
        out_shape=[jax.ShapeDtypeStruct((rows, columns), BF16), jax.ShapeDtypeStruct((rows, width), BF16)],
        compiler_params=pltpu.CompilerParams(vmem_limit_bytes=VMEM_LIMIT),
        cost_estimate=pl.CostEstimate(
            flops=2 * rows * width * columns,
            bytes_accessed=2 * (rows * (2 * width + columns) + width * columns),
            transcendentals=rows,
        ),
        name="project",
    )(x, gain, bias, weight, add, cos_tab, sin_tab)


def head_parts(rows, factor):
    rows = rows.astype(F32) * factor
    lane = lax.broadcasted_iota(jnp.int32, rows.shape, 1)
    first = lane < HEAD_DIM
    return (jnp.where(first, rows, 0.0).astype(BF16), jnp.where(first, 0.0, rows).astype(BF16))


def flipped(tile):
    return tile.astype(F32).T.astype(BF16)


def nt_dot(a, b):
    return lax.dot_general(a, b, NT, preferred_element_type=F32)


def own_mask(limit_ref, noisy_rows, rows):
    at = lax.broadcasted_iota(jnp.int32, (noisy_rows, rows), 0)
    return (at >= limit_ref[1:2, :]) & (at < limit_ref[2:3, :])


def attend_kernel(count_ref, q_ref, kn_ref, vn_ref, kc_ref, vc_ref, limit_ref, o_ref, log_ref, *, block):
    rows = q_ref.shape[0]
    queries = head_parts(q_ref[...], SCALE)
    limit = limit_ref[0:1, :]

    def fold(state, keys, values, mask):
        values_flipped = flipped(values)
        out = []
        for h in range(2):
            best, total, acc = state[h]
            scores = jnp.where(mask, nt_dot(keys, queries[h]), NEGATIVE)
            new_best = jnp.maximum(best, jnp.max(scores, 0, keepdims=True))
            weights = jnp.exp(scores - new_best)
            factor = jnp.exp(best - new_best)
            total = total * factor + jnp.sum(weights, 0, keepdims=True)
            acc = acc * factor + jnp.dot(
                values_flipped[h * HEAD_DIM : (h + 1) * HEAD_DIM], weights.astype(BF16), preferred_element_type=F32
            )
            out.append((new_best, total, acc))
        return tuple(out)

    def step(index, state):
        first = pl.multiple_of(index * block, block)
        at = lax.broadcasted_iota(jnp.int32, (block, rows), 0) + index * block
        return fold(state, kc_ref[pl.ds(first, block), :], vc_ref[pl.ds(first, block), :], at < limit)

    start = (
        jnp.full((1, rows), NEGATIVE, F32),
        jnp.zeros((1, rows), F32),
        jnp.zeros((HEAD_DIM, rows), F32),
    )
    state = lax.fori_loop(0, count_ref[0], step, (start, start))
    state = fold(state, kn_ref[...], vn_ref[...], own_mask(limit_ref, kn_ref.shape[0], rows))
    o_ref[...] = jnp.concatenate([acc / total for _, total, acc in state], 0).T.astype(BF16)
    for h in range(2):
        log_ref[0, h : h + 1, :] = state[h][0] + jnp.log(state[h][1])


def attend(count, own, clean, limits, block):
    rows = own.shape[0]
    length = clean.shape[0]
    pairs = own.shape[1] // (3 * LANES)
    spec = pltpu.PrefetchScalarGridSpec(
        num_scalar_prefetch=1,
        grid=(pairs,),
        in_specs=[
            pl.BlockSpec((rows, LANES), lambda p, c: (0, p)),
            pl.BlockSpec((rows // 2, LANES), lambda p, c: (0, pairs + p)),
            pl.BlockSpec((rows // 2, LANES), lambda p, c: (0, 2 * pairs + p)),
            pl.BlockSpec((length, LANES), lambda p, c: (0, p)),
            pl.BlockSpec((length, LANES), lambda p, c: (0, pairs + p)),
            pl.BlockSpec((8, rows), lambda p, c: (0, 0)),
        ],
        out_specs=[
            pl.BlockSpec((rows, LANES), lambda p, c: (0, p)),
            pl.BlockSpec((1, 8, rows), lambda p, c: (p, 0, 0)),
        ],
    )
    return pl.pallas_call(
        functools.partial(attend_kernel, block=block),
        grid_spec=spec,
        out_shape=[
            jax.ShapeDtypeStruct((rows, pairs * LANES), BF16),
            jax.ShapeDtypeStruct((pairs, 8, rows), F32),
        ],
        compiler_params=pltpu.CompilerParams(vmem_limit_bytes=VMEM_LIMIT),
        cost_estimate=pl.CostEstimate(
            flops=pairs * rows * (length + rows // 2) * 2048,
            bytes_accessed=2 * pairs * LANES * (2 * length + 3 * rows),
            transcendentals=2 * pairs * rows * length,
        ),
        name="attend",
    )(count, own, own, own, clean, clean, limits)


def attend_back_kernel(
    count_ref, q_ref, kn_ref, vn_ref, kc_ref, vc_ref, limit_ref, o_ref, do_ref, log_ref,
    cos_own_ref, sin_own_ref, cos_ref, sin_ref, dkv_ref, down_ref, sum_ref, *, block
):
    rows = q_ref.shape[0]
    noisy = kn_ref.shape[0]
    width = dkv_ref.shape[1] // 2
    length = kc_ref.shape[0]
    here = pl.multiple_of(pl.program_id(0) * LANES, LANES)
    queries = head_parts(q_ref[...], SCALE)
    grads = head_parts(do_ref[...], 1.0)
    limit = limit_ref[0:1, :]
    product = do_ref[...].astype(F32) * o_ref[...].astype(F32)
    lane = lax.broadcasted_iota(jnp.int32, (8, LANES), 1)
    deltas = []
    for h in range(2):
        ones = jnp.where((lane < HEAD_DIM) == (h == 0), 1.0, 0.0)
        deltas.append(
            lax.dot_general(ones, product, NT, precision=lax.Precision.HIGHEST, preferred_element_type=F32)[0:1]
        )

    def fold(dq, keys, values, mask):
        keys_flipped = flipped(keys)
        dk = dv = None
        out = []
        for h in range(2):
            scores = nt_dot(keys, queries[h])
            probs = jnp.where(mask, jnp.exp(scores - log_ref[0, h : h + 1, :]), 0.0)
            inner = nt_dot(values, grads[h])
            slopes = (probs * (inner - deltas[h])).astype(BF16)
            dv_new = jnp.dot(probs.astype(BF16), grads[h], preferred_element_type=F32)
            dk_new = jnp.dot(slopes, queries[h], preferred_element_type=F32)
            dv = dv_new if dv is None else dv + dv_new
            dk = dk_new if dk is None else dk + dk_new
            out.append(
                dq[h]
                + jnp.dot(keys_flipped[h * HEAD_DIM : (h + 1) * HEAD_DIM], slopes, preferred_element_type=F32)
            )
        return tuple(out), dk, dv

    def unturn(grad, cos_tab, sin_tab):
        return grad * cos_tab - swap_halves(grad) * sin_tab

    def step(index, carry):
        dq, sum_k, sum_v = carry
        first = pl.multiple_of(index * block, block)
        where = pl.ds(first, block)
        at = lax.broadcasted_iota(jnp.int32, (block, rows), 0) + index * block
        dq, dk, dv = fold(dq, kc_ref[where, :], vc_ref[where, :], at < limit)
        dk = unturn(dk, cos_ref[where, :], sin_ref[where, :])
        dkv_ref[where, pl.ds(here, LANES)] = dk.astype(BF16)
        dkv_ref[where, pl.ds(width + here, LANES)] = dv.astype(BF16)
        return dq, sum_k + jnp.sum(dk, 0, keepdims=True), sum_v + jnp.sum(dv, 0, keepdims=True)

    zero_q = jnp.zeros((HEAD_DIM, rows), F32)
    zero_sum = jnp.zeros((1, LANES), F32)
    dq, sum_k, sum_v = lax.fori_loop(0, count_ref[0], step, ((zero_q, zero_q), zero_sum, zero_sum))

    def blank(index, carry):
        where = pl.ds(pl.multiple_of(index * block, block), block)
        dkv_ref[where, pl.ds(here, LANES)] = jnp.zeros((block, LANES), BF16)
        dkv_ref[where, pl.ds(width + here, LANES)] = jnp.zeros((block, LANES), BF16)
        return carry

    lax.fori_loop(count_ref[0], length // block, blank, 0)
    dq, dk, dv = fold(dq, kn_ref[...], vn_ref[...], own_mask(limit_ref, noisy, rows))
    dk = unturn(dk, cos_own_ref[:noisy, :], sin_own_ref[:noisy, :])
    dq = unturn(jnp.concatenate(dq, 0).T * SCALE, cos_own_ref[...], sin_own_ref[...])
    zeros = jnp.zeros((rows - noisy, LANES), BF16)
    for part, grad in enumerate((dq, dk, dv)):
        down_ref[: grad.shape[0], pl.ds(part * width + here, LANES)] = grad.astype(BF16)
        if part > 0:
            down_ref[noisy:, pl.ds(part * width + here, LANES)] = zeros
    sums = (
        jnp.sum(dq, 0, keepdims=True),
        sum_k + jnp.sum(dk, 0, keepdims=True),
        sum_v + jnp.sum(dv, 0, keepdims=True),
    )
    for part in range(3):
        sum_ref[:, pl.ds(part * width + here, LANES)] = jnp.broadcast_to(sums[part], (8, LANES))


def attend_back(count, own, clean, limits, attn, grad, log_total, cos_own, sin_own, cos_tab, sin_tab, block):
    rows = own.shape[0]
    length, both = clean.shape
    pairs = own.shape[1] // (3 * LANES)
    spec = pltpu.PrefetchScalarGridSpec(
        num_scalar_prefetch=1,
        grid=(pairs,),
        in_specs=[
            pl.BlockSpec((rows, LANES), lambda p, c: (0, p)),
            pl.BlockSpec((rows // 2, LANES), lambda p, c: (0, pairs + p)),
            pl.BlockSpec((rows // 2, LANES), lambda p, c: (0, 2 * pairs + p)),
            pl.BlockSpec((length, LANES), lambda p, c: (0, p)),
            pl.BlockSpec((length, LANES), lambda p, c: (0, pairs + p)),
            pl.BlockSpec((8, rows), lambda p, c: (0, 0)),
            pl.BlockSpec((rows, LANES), lambda p, c: (0, p)),
            pl.BlockSpec((rows, LANES), lambda p, c: (0, p)),
            pl.BlockSpec((1, 8, rows), lambda p, c: (p, 0, 0)),
            pl.BlockSpec((rows, LANES), lambda p, c: (0, 0)),
            pl.BlockSpec((rows, LANES), lambda p, c: (0, 0)),
            pl.BlockSpec((length, LANES), lambda p, c: (0, 0)),
            pl.BlockSpec((length, LANES), lambda p, c: (0, 0)),
        ],
        out_specs=[
            pl.BlockSpec((length, both), lambda p, c: (0, 0)),
            pl.BlockSpec((rows, own.shape[1]), lambda p, c: (0, 0)),
            pl.BlockSpec((8, own.shape[1]), lambda p, c: (0, 0)),
        ],
    )
    return pl.pallas_call(
        functools.partial(attend_back_kernel, block=block),
        grid_spec=spec,
        out_shape=[
            jax.ShapeDtypeStruct((length, both), BF16),
            jax.ShapeDtypeStruct(own.shape, BF16),
            jax.ShapeDtypeStruct((8, own.shape[1]), F32),
        ],
        compiler_params=pltpu.CompilerParams(vmem_limit_bytes=VMEM_LIMIT),
        cost_estimate=pl.CostEstimate(
            flops=pairs * rows * (length + rows // 2) * 5120,
            bytes_accessed=2 * pairs * LANES * (5 * length + 8 * rows),
            transcendentals=2 * pairs * rows * length,
        ),
        name="attend_back",
    )(count, own, own, own, clean, clean, limits, attn, grad, log_total, cos_own, sin_own, cos_tab, sin_tab)


def feed_forward_kernel(
    attn_ref, x_ref, top_ref, up_ref, down_ref, out_ref, vec_ref,
    block_out_ref, hidden_grad_ref, attn_grad_ref, weights_ref,
    hidden, unit, inverse, normed, normed_flipped, lowered, grad_normed,
    up_grads, down_grads, out_grads, vec_grads, sums, up_sems, down_sems, last_sems
):
    chunk = pl.program_id(0)
    chunks = pl.num_programs(0)
    width = x_ref.shape[1]

    @pl.when(chunk == 0)
    def _():
        value = (
            x_ref[...].astype(F32)
            + jnp.dot(attn_ref[...], out_ref[...], preferred_element_type=F32)
            + vec_ref[0:1, :]
        )
        hidden[...] = value
        center = value - jnp.mean(value, -1, keepdims=True)
        scale = lax.rsqrt(jnp.mean(center * center, -1, keepdims=True) + EPSILON)
        inverse[...] = scale
        unit[...] = center * scale
        scaled = unit[...] * vec_ref[1:2, :] + vec_ref[2:3, :]
        normed[...] = scaled.astype(BF16)
        normed_flipped[...] = scaled.T.astype(BF16)
        lowered[...] = jnp.zeros_like(lowered)
        grad_normed[...] = jnp.zeros_like(grad_normed)
        sums[...] = jnp.zeros_like(sums)

    upper = jnp.dot(normed[...], up_ref[...], preferred_element_type=F32) + vec_ref[pl.ds(4 + chunk, 1), :]
    grad_activ = nt_dot(top_ref[...], down_ref[...])
    inner = jnp.tanh(0.7978845608028654 * (upper + 0.044715 * upper * upper * upper))
    activ = 0.5 * upper * (1.0 + inner)
    slope = 0.5 * (1.0 + inner) + 0.5 * upper * (1.0 - inner * inner) * 0.7978845608028654 * (
        1.0 + 0.134145 * upper * upper
    )
    grad_upper = grad_activ * slope
    grad_low = grad_upper.astype(BF16)
    sums[pl.ds(4 + chunk, 1), :] = jnp.sum(grad_upper, 0, keepdims=True)
    lowered[...] += jnp.dot(activ.astype(BF16), down_ref[...], preferred_element_type=F32)
    grad_normed[...] += nt_dot(grad_low, up_ref[...])
    up_grads[chunk] = jnp.dot(normed_flipped[...], grad_low, preferred_element_type=F32).astype(BF16)
    down_grads[chunk] = jnp.dot(activ.T.astype(BF16), top_ref[...], preferred_element_type=F32).astype(BF16)

    def copy_up(index):
        columns = pl.ds(pl.multiple_of(index * width, width), width)
        return pltpu.make_async_copy(up_grads.at[index], weights_ref.at[:, columns], up_sems.at[index])

    def copy_down(index):
        columns = pl.ds(pl.multiple_of((chunks + index) * width, width), width)
        return pltpu.make_async_copy(down_grads.at[index], weights_ref.at[:, columns], down_sems.at[index])

    copy_up(chunk).start()
    copy_down(chunk).start()

    @pl.when(chunk == chunks - 1)
    def _():
        top = top_ref[...].astype(F32)
        block_out_ref[...] = (hidden[...] + lowered[...] + vec_ref[3:4, :]).astype(BF16)
        grad = grad_normed[...]
        rows_unit = unit[...]
        sums[1:2, :] = jnp.sum(grad * rows_unit, 0, keepdims=True)
        sums[2:3, :] = jnp.sum(grad, 0, keepdims=True)
        sums[3:4, :] = jnp.sum(top, 0, keepdims=True)
        grad = grad * vec_ref[1:2, :]
        grad = inverse[...] * (
            grad - jnp.mean(grad, -1, keepdims=True) - rows_unit * jnp.mean(grad * rows_unit, -1, keepdims=True)
        )
        grad = top + grad
        hidden_grad_ref[...] = grad
        sums[0:1, :] = jnp.sum(grad, 0, keepdims=True)
        low = grad.astype(BF16)
        attn_grad_ref[...] = nt_dot(low, out_ref[...]).astype(BF16)
        out_grads[...] = jnp.dot(
            attn_ref[...].astype(F32).T.astype(BF16), low, preferred_element_type=F32
        ).astype(BF16)
        vec_grads[...] = sums[...].T.astype(BF16)
        first = 2 * chunks * width
        copies = [
            pltpu.make_async_copy(out_grads, weights_ref.at[:, pl.ds(first, width)], last_sems.at[0]),
            pltpu.make_async_copy(vec_grads, weights_ref.at[:, pl.ds(first + width, LANES)], last_sems.at[1]),
        ]
        for copy in copies:
            copy.start()
        for index in range(up_grads.shape[0]):
            copy_up(index).wait()
            copy_down(index).wait()
        for copy in copies:
            copy.wait()


def feed_forward(attn, x, top, weights, vectors, chunks):
    rows, width = x.shape
    fixed = lambda b: (0, 0)
    whole = pl.BlockSpec((rows, width), fixed)
    return pl.pallas_call(
        feed_forward_kernel,
        grid=(chunks,),
        in_specs=[
            whole,
            whole,
            whole,
            pl.BlockSpec((width, width), lambda b: (0, b)),
            pl.BlockSpec((width, width), lambda b: (0, chunks + b)),
            pl.BlockSpec((width, width), lambda b: (0, 2 * chunks)),
            pl.BlockSpec(vectors.shape, fixed),
        ],
        out_specs=[whole, whole, whole, pl.BlockSpec(memory_space=pl.ANY)],
        out_shape=[
            jax.ShapeDtypeStruct((rows, width), BF16),
            jax.ShapeDtypeStruct((rows, width), F32),
            jax.ShapeDtypeStruct((rows, width), BF16),
            jax.ShapeDtypeStruct(weights.shape, BF16),
        ],
        scratch_shapes=[
            pltpu.VMEM((rows, width), F32),
            pltpu.VMEM((rows, width), F32),
            pltpu.VMEM((rows, 1), F32),
            pltpu.VMEM((rows, width), BF16),
            pltpu.VMEM((width, rows), BF16),
            pltpu.VMEM((rows, width), F32),
            pltpu.VMEM((rows, width), F32),
            pltpu.VMEM((chunks, width, width), BF16),
            pltpu.VMEM((chunks, width, width), BF16),
            pltpu.VMEM((width, width), BF16),
            pltpu.VMEM((width, LANES), BF16),
            pltpu.VMEM((LANES, width), F32),
            pltpu.SemaphoreType.DMA((chunks,)),
            pltpu.SemaphoreType.DMA((chunks,)),
            pltpu.SemaphoreType.DMA((2,)),
        ],
        compiler_params=pltpu.CompilerParams(vmem_limit_bytes=VMEM_LIMIT),
        cost_estimate=pl.CostEstimate(
            flops=2 * rows * width * width * (6 * chunks + 3),
            bytes_accessed=4 * width * weights.shape[1] + 12 * rows * width,
            transcendentals=rows * width * chunks,
        ),
        name="feed_forward",
    )(attn, x, top, weights, weights, weights, vectors)


def pick(array, index, axis=0):
    return lax.dynamic_index_in_dim(array, index, axis, keepdims=False)


def ordered(flag, own, other, axis):
    return jnp.stack([jnp.where(flag == 0, own, other), jnp.where(flag == 0, other, own)], axis)


class Links:
    def __init__(self):
        self.count = lax.axis_size("ctx")
        self.deep = self.count // 4
        at = lax.axis_index("ctx")
        self.x = lax.axis_index("batch")
        self.core = at % 2
        self.y = (at // 2) % 2
        self.z = at // 4
        self.chip = at // 2

    def over_core(self, array):
        return lax.ppermute(array, "ctx", [(i, i ^ 1) for i in range(self.count)])

    def over_y(self, array):
        return lax.ppermute(array, "ctx", [(i, i ^ 2) for i in range(self.count)])

    def over_x(self, array):
        return lax.ppermute(array, "batch", [(0, 1), (1, 0)])

    def along_z(self, array, hop):
        count = self.count
        return lax.ppermute(array, "ctx", [(i, (i + 4 * hop) % count) for i in range(count)])

    def gather_z(self, piece):
        deep = self.deep
        whole = jnp.broadcast_to(piece[None], (deep,) + piece.shape)
        for hop in range(1, deep):
            whole = lax.dynamic_update_index_in_dim(whole, self.along_z(piece, hop), (self.z - hop) % deep, 0)
        return whole

    def gather_plane(self, piece):
        column = self.gather_z(piece)
        return ordered(self.y, column, self.over_y(column), 1)

    def gather(self, piece):
        plane = self.gather_plane(piece)
        return ordered(self.x, plane, self.over_x(plane), 0)

    def reduce_z(self, parts):
        total = pick(parts, self.z).astype(F32)
        for hop in range(1, self.deep):
            total = total + self.along_z(pick(parts, (self.z + hop) % self.deep), hop).astype(F32)
        return total

    def reduce_plane(self, parts):
        got = self.over_y(pick(parts, 1 - self.y, 1))
        mine = pick(parts, self.y, 1)
        return self.reduce_z((mine.astype(F32) + got.astype(F32)).astype(BF16))

    def reduce(self, parts):
        got = self.over_x(pick(parts, 1 - self.x))
        mine = pick(parts, self.x)
        return self.reduce_plane((mine.astype(F32) + got.astype(F32)).astype(BF16))


def unit_rows(values):
    center = values - jnp.mean(values, -1, keepdims=True)
    spread = jnp.mean(center * center, -1, keepdims=True)
    inverse = lax.rsqrt(spread + EPSILON)
    return center * inverse, inverse


def unit_back(grad, unit, inverse):
    return inverse * (
        grad - jnp.mean(grad, -1, keepdims=True) - unit * jnp.mean(grad * unit, -1, keepdims=True)
    )


def rotary_tables(positions):
    half_dim = HEAD_DIM // 2
    inverse = 1.0 / THETA ** (jnp.arange(half_dim, dtype=F32) / half_dim)
    angles = positions.astype(F32)[:, None] * jnp.tile(inverse, LANES // half_dim)[None, :]
    sign = jnp.where(jnp.arange(LANES) % HEAD_DIM < half_dim, -1.0, 1.0)
    return jnp.cos(angles), jnp.sin(angles) * sign[None, :]


def key_block(length):
    for block in (256, 128, 64, 32, 16):
        if length % block == 0:
            return block
    return length


def row_block(rows):
    for block in (512, 384, 256, 128, 64, 32, 16):
        if rows % block == 0:
            return block
    return rows


def dot(a, b):
    return jnp.dot(a, b, preferred_element_type=F32)


def dot_left(a, b):
    return lax.dot_general(a, b, (((0,), (0,)), ((), ())), preferred_element_type=F32)


def on_device(
    layer_input, cotangent, prefix, block_size, ln1_gain, ln1_bias, qkv_weight, qkv_bias, out_weight, out_bias,
    ln2_gain, ln2_bias, up_weight, up_bias, down_weight, down_bias,
):
    links = Links()
    core = links.core
    seqs, _, pos_dev, width = layer_input.shape
    devices = 2 * links.count
    length = links.count * pos_dev
    half = width // 2
    rows = 4 * pos_dev
    shard = ln1_gain.shape[0]
    hidden_shard = up_bias.shape[0]

    folds = hidden_shard // shard
    up_piece = up_weight.reshape(shard, devices, folds, shard).transpose(0, 2, 1, 3).reshape(shard, -1)
    down_piece = down_weight.reshape(folds, shard, width).transpose(1, 0, 2).reshape(shard, -1)
    vec_piece = jnp.stack(
        [out_bias, ln2_gain, ln2_bias, down_bias] + [up_bias[i * shard : (i + 1) * shard] for i in range(folds)], 1
    )
    vec_piece = jnp.pad(vec_piece, ((0, 0), (0, LANES - vec_piece.shape[1])))
    packed = jnp.concatenate([up_piece, down_piece, out_weight, vec_piece], 1)
    weights = lax.all_gather(packed, ("batch", "ctx"), axis=0, tiled=True)
    vectors = weights[:, -LANES:].T[: 4 + folds].astype(F32)

    split = qkv_weight.reshape(shard, 3, 2, half)
    vec_one = jnp.stack([ln1_gain, ln1_bias] + [qkv_bias[i * shard : (i + 1) * shard] for i in range(3)], 1)
    vec_one = jnp.pad(vec_one, ((0, 0), (0, LANES - vec_one.shape[1])))
    mine = jnp.concatenate([pick(split, core, 2).reshape(shard, 3 * half), vec_one], 1)
    theirs = jnp.concatenate([pick(split, 1 - core, 2).reshape(shard, 3 * half), vec_one], 1)
    piece = ordered(core, mine, links.over_core(theirs), 0).reshape(2 * shard, -1)
    qkv_mat = links.gather(piece).reshape(width, -1)
    vec_one = qkv_mat[:, 3 * half :].T.astype(F32)
    gain_one, bias_one = vec_one[0:1], vec_one[1:2]
    qkv_add = vec_one[2:5].reshape(3, devices, shard).transpose(1, 0, 2).reshape(3, 2, half)
    qkv_add = pick(qkv_add, core, 1).reshape(1, 3 * half)
    qkv_mat = qkv_mat[:, : 3 * half]

    lane_rows = links.gather_plane(layer_input[:, 1])
    lane_rows = ordered(core, lane_rows, links.over_core(lane_rows), 3)
    clean_inputs = lane_rows.transpose(2, 0, 1, 3, 4, 5).reshape(seqs, length, width)

    inputs_pair = ordered(core, layer_input, links.over_core(layer_input), 2).reshape(seqs, rows, width)

    cos_tab, sin_tab = rotary_tables(jnp.arange(length, dtype=jnp.int32))
    first_pos = links.chip * 2 * pos_dev
    cos_own = jnp.tile(lax.dynamic_slice_in_dim(cos_tab, first_pos, 2 * pos_dev, 0), (2, 1))
    sin_own = jnp.tile(lax.dynamic_slice_in_dim(sin_tab, first_pos, 2 * pos_dev, 0), (2, 1))
    block = key_block(length)
    at = jnp.arange(2 * pos_dev, dtype=jnp.int32)
    position = first_pos + at
    own_qkv, own_unit, clean_kv, clean_unit, limit_list, counts, attn_list, log_list = ([] for _ in range(8))
    for s in range(seqs):
        near = (position // block_size[s]) * block_size[s]
        after = near + block_size[s]
        noisy_limit = jnp.maximum(near, prefix[s])
        clean_limit = jnp.where(position < prefix[s], prefix[s], after)
        limit = jnp.concatenate([noisy_limit, clean_limit])
        none = jnp.zeros_like(at)
        limits = jnp.stack(
            [limit, jnp.concatenate([near - first_pos, none]), jnp.concatenate([after - first_pos, none])]
            + [jnp.zeros_like(limit)] * 5
        )
        count = jnp.minimum((jnp.max(limit) + block - 1) // block, length // block).reshape(1)
        own, unit = project(
            inputs_pair[s], gain_one, bias_one, qkv_mat, qkv_add, cos_own, sin_own, 0, width, row_block(rows)
        )
        clean, all_unit = project(
            clean_inputs[s], gain_one, bias_one, qkv_mat, qkv_add, cos_tab, sin_tab, half, half, row_block(length)
        )
        attn, log_total = attend(count, own, clean, limits, block)
        for kept, value in zip(
            (own_qkv, own_unit, clean_kv, clean_unit, limit_list, counts, attn_list, log_list),
            (own, unit, clean, all_unit, limits, count, attn, log_total),
        ):
            kept.append(value)

    attn_rows = jnp.stack(attn_list).reshape(seqs, 2, 2, pos_dev, half)
    attn_got = links.over_core(pick(attn_rows, 1 - core, 2))
    attn_low = ordered(core, pick(attn_rows, core, 2), attn_got, 3).reshape(-1, width)
    flat_inputs = layer_input.reshape(-1, width)
    output, grad_hidden, grad_attn, weight_grads = feed_forward(
        attn_low, flat_inputs, cotangent.reshape(-1, width), weights, vectors, folds
    )
    output = output.reshape(layer_input.shape)
    packed = lax.psum_scatter(weight_grads, ("batch", "ctx"), scatter_dimension=0, tiled=True).astype(F32)

    grad_split = grad_attn.reshape(-1, 2, half)
    grad_got = links.over_core(pick(grad_split, 1 - core, 1))
    grad_rows = ordered(
        core,
        pick(grad_split, core, 1).reshape(seqs, 2, pos_dev, half),
        grad_got.reshape(seqs, 2, pos_dev, half),
        2,
    ).reshape(seqs, rows, half)
    clean_grads, own_grads, column_sums = [], [], 0.0
    for s in range(seqs):
        clean_grad, own_grad, sums = attend_back(
            counts[s], own_qkv[s], clean_kv[s], limit_list[s], attn_list[s], grad_rows[s], log_list[s],
            cos_own, sin_own, cos_tab, sin_tab, block,
        )
        clean_grads.append(clean_grad)
        own_grads.append(own_grad)
        column_sums = column_sums + sums[0]

    kv_mat = qkv_mat[:, half:]
    spread, local = [], []
    for s in range(seqs):
        spread.append(lax.dot_general(clean_grads[s], kv_mat, NT, preferred_element_type=F32).astype(BF16))
        local.append(lax.dot_general(own_grads[s], qkv_mat, NT, preferred_element_type=F32).astype(BF16))
    spread = jnp.stack([part.reshape(links.deep, 2, 2, pos_dev, width) for part in spread], 2)
    local = jnp.stack([part.reshape(2, 2, pos_dev, width) for part in local])
    spread = pick(spread, core, 3).astype(F32) + links.over_core(pick(spread, 1 - core, 3)).astype(F32)
    local = pick(local, core, 2).astype(F32) + links.over_core(pick(local, 1 - core, 2)).astype(F32)
    total = links.reduce_plane(spread.astype(BF16))
    grad_normed_one = jnp.stack([local[:, 0], local[:, 1] + total], 1).reshape(-1, width)
    unit_one, inverse_one = unit_rows(flat_inputs.astype(F32))
    grad_input = grad_hidden + unit_back(grad_normed_one * gain_one, unit_one, inverse_one)
    grad_input = grad_input.astype(BF16).reshape(layer_input.shape)

    unit_part = jnp.zeros((width, 3 * half), F32)
    kv_part = jnp.zeros((width, 2 * half), F32)
    for s in range(seqs):
        unit_part = unit_part + dot_left(own_unit[s], own_grads[s])
        kv_part = kv_part + dot_left(clean_unit[s], clean_grads[s])
    unit_part = unit_part + jnp.pad(kv_part, ((0, 0), (half, 0)))
    wide = qkv_mat.astype(F32)
    gain_part = jnp.sum(wide * unit_part, -1)
    bias_part = jnp.sum(wide * column_sums[None, :], -1)
    qkv_part = gain_one.reshape(-1, 1) * unit_part + bias_one.reshape(-1, 1) * column_sums[None, :]
    column_sums = ordered(core, column_sums.reshape(3, half), jnp.zeros((3, half), F32), 1).reshape(3 * width)
    qk_part = column_sums[: 2 * width].reshape(devices, 2, shard).transpose(0, 2, 1).reshape(width, 2)
    vec_part = jnp.concatenate(
        [jnp.stack([gain_part, bias_part, column_sums[2 * width :]], 1), qk_part], 1
    )
    vec_part = jnp.pad(vec_part, ((0, 0), (0, LANES - vec_part.shape[1])))
    qkv_part = jnp.concatenate([qkv_part, vec_part], 1).astype(BF16)
    qkv_sum = links.reduce(qkv_part.reshape(2, links.deep, 2, 2 * shard, -1)).reshape(2, shard, -1)
    qkv_mine = pick(qkv_sum, core)
    qkv_got = links.over_core(pick(qkv_sum, 1 - core))
    grad_qkv = ordered(
        core, qkv_mine[:, : 3 * half].reshape(shard, 3, half), qkv_got[:, : 3 * half].reshape(shard, 3, half), 2
    ).reshape(shard, 3 * width)
    vec_sum = (qkv_mine[:, 3 * half :] + qkv_got[:, 3 * half :]).T

    hidden_width = devices * hidden_shard
    grad_up = packed[:, :hidden_width].reshape(shard, folds, devices, shard).transpose(0, 2, 1, 3)
    grad_up = grad_up.reshape(shard, hidden_width)
    grad_down = packed[:, hidden_width : hidden_width + folds * width].reshape(shard, folds, width)
    grad_down = grad_down.transpose(1, 0, 2).reshape(hidden_shard, width)
    grad_out = packed[:, hidden_width + folds * width : -LANES]
    late = packed[:, -LANES:].T

    return (
        output, grad_input, vec_sum[0], vec_sum[1], grad_qkv, vec_sum[3:5].reshape(-1), vec_sum[2], grad_out,
        late[0], late[1], late[2], grad_up, late[4 : 4 + folds].reshape(-1), grad_down, late[3],
    )


def solution(mesh):
    every = P(("batch", "ctx"))
    matrix = P(("batch", "ctx"), None)
    acts = P("batch", None, "ctx", None)
    return jax.shard_map(
        on_device,
        mesh=mesh,
        in_specs=(
            acts, acts, P("batch"), P("batch"), every, every, matrix, every, matrix, every, every, every, matrix,
            every, matrix, every,
        ),
        out_specs=(
            acts, acts, every, every, matrix, every, every, matrix, every, every, every, matrix, every, matrix, every,
        ),
        check_vma=False,
    )
```

time: 1310 us -> 455 us (0.35)
  the two profiles are of different devices: /device:TPU:0 before, /device:TPU:8 now
where the time goes in v1:
time: 455 us; the launch traced here: 449 us
  waiting for transfers between devices  151 us (33%)
  Pallas kernels  101 us (22%)
  local copies, waits for them, and re-layouts  61.4 us (13%)
  starting transfers between devices  53 us (12%)
  other arithmetic  45.6 us (10%)
  between operations  19.8 us (4%)
  matrix products  16.4 us (4%)
    ppermute x12, waiting for transfers between devices, along_z(): lax.ppermute(array, 'ctx', [(i, (i + 4 * hop) % count) for i in range(cou...  66.3 us
    ppermute x4, waiting for transfers between devices, over_y(): return lax.ppermute(array, 'ctx', [(i, i ^ 2) for i in range(self.count)])  60.5 us
    ppermute x12, starting transfers between devices, along_z(): lax.ppermute(array, 'ctx', [(i, (i + 4 * hop) % count) for i in range(cou...  40 us
    pallas_call x2, Pallas kernels, attend_back(): pl.pallas_call(functools.partial(attend_back_kernel, block=block), grid_s...  34.8 us
    pallas_call x1, Pallas kernels, feed_forward(): pl.pallas_call(feed_forward_kernel, grid=(chunks,), in_specs=[whole, whol...  23.1 us
    pallas_call x2, Pallas kernels, attend(): pl.pallas_call(functools.partial(attend_kernel, block=block), grid_spec=s...  21.8 us
    pallas_call x4, Pallas kernels, project(): pl.pallas_call(functools.partial(project_kernel, start=start, turned=turn...  21.8 us
    ppermute x2, waiting for transfers between devices, over_x(): return lax.ppermute(array, 'batch', [(0, 1), (1, 0)])  21.5 us
  transfers between devices with their start and end apart: 28, of which 16 were waited for; matrix products, arithmetic and copies ran while one was open for 22% of the time, Pallas kernels for 17%

profile of v1, /device:TPU:8, one launch (start us, length us, event | category | flops | bytes accessed | tf_op | source)
XLA Modules:
  0.0 448.6 jit_solution(6483424327023623659)
XLA Ops:
  33.6 16.7 %collective-permute-done.2 = bf16[48,1280]{1,0:T(8,128)(2,1)S(1)} collective-permute-done((bf16[48,1280]{1,0:T(8,128)(2,1)S(1)}, bf16[48,1280]{1,0:T(8,128)(2,1)S(1)}, u32[]{:S(2)}, u32[]{:S(2)}) %collective-permute-start.2) | collective-permute-done | bytes 122912 | tf_op jit(solution)/shard_map/ppermute | solution.py:467
  52.4 9.7 %collective-permute-done.3 = bf16[48,1280]{1,0:T(8,128)(2,1)S(1)} collective-permute-done((bf16[48,1280]{1,0:T(8,128)(2,1)S(1)}, bf16[48,1280]{1,0:T(8,128)(2,1)S(1)}, u32[]{:S(2)}, u32[]{:S(2)}) %collective-permute-start.3) | collective-permute-done | bytes 122912 | tf_op jit(solution)/shard_map/ppermute | solution.py:467
  62.1 8.2 %collective-permute-done.4 = bf16[48,1280]{1,0:T(8,128)(2,1)S(1)} collective-permute-done((bf16[48,1280]{1,0:T(8,128)(2,1)S(1)}, bf16[48,1280]{1,0:T(8,128)(2,1)S(1)}, u32[]{:S(2)}, u32[]{:S(2)}) %collective-permute-start.4) | collective-permute-done | bytes 122912 | tf_op jit(solution)/shard_map/ppermute | solution.py:467
  72.7 4.9 %fusion.25 = (f32[1536,128]{1,0:T(8,128)}, f32[1536,128]{1,0:T(8,128)}) fusion(f32[128]{0:T(128)S(1)} %compare_select_fusion.1, f32[128]{0:T(128)S(1)} %mul.211, f32[1536]{0:T(1024)S(1)} %iota_convert_fusion), kind=kLoop, calls=%fused_computation.73 | loop fusion | flops 393216 | bytes 1580032 | tf_op jit(solution)/shard_map/mul | solution.py:519
  77.5 7.0 %collective-permute-done.5 = bf16[4,48,1280]{2,1,0:T(8,128)(2,1)S(1)} collective-permute-done((bf16[4,48,1280]{2,1,0:T(8,128)(2,1)S(1)}, bf16[4,48,1280]{2,1,0:T(8,128)(2,1)S(1)}, u32[]{:S(2)}, u32[]{:S(2)}) %collective-permute-start.5) | collective-permute-done | bytes 491552 | tf_op jit(solution)/shard_map/ppermute | solution.py:460
  85.7 4.9 %collective-permute-start.6 = (bf16[4,2,48,1280]{3,2,1,0:T(8,128)(2,1)}, bf16[4,2,48,1280]{3,2,1,0:T(8,128)(2,1)}, u32[]{:S(2)}, u32[]{:S(2)}) collective-permute-start(bf16[4,2,48,1280]{3,2,1,0:T(8,128)(2,1)} %pad_maximum_fusion.3), channel_id=1, source_target_pairs={{0,16},{16,0},{1,17},{17,1},{2,18},{18,2},{3,19},{19,3},{4,20},{20... | collective-permute-start | bytes 2949128 | tf_op jit(solution)/shard_map/ppermute | solution.py:463
  90.6 35.7 %collective-permute-done.10 = bf16[4,2,96,768]{3,2,0,1:T(8,128)(2,1)S(1)} collective-permute-done((bf16[4,2,96,768]{3,2,0,1:T(8,128)(2,1)S(1)}, bf16[4,2,96,768]{3,2,0,1:T(8,128)(2,1)S(1)}, u32[]{:S(2)}, u32[]{:S(2)}) %collective-permute-start.10) | collective-permute-done | bytes 1179680 | tf_op jit(solution)/shard_map/ppermute | solution.py:460
  146.9 3.9 project.6
  150.9 3.9 project.4
  157.2 2.6 fusion.58
  159.8 6.9 %project.7 = (bf16[1536,768]{1,0:T(8,128)(2,1)}, bf16[1536,768]{1,0:T(8,128)(2,1)}) custom-call(bf16[1536,768]{1,0:T(8,128)(2,1)} %bitcast.257, f32[1,768]{1,0:T(1,128)} %copy.308.gain_ref, f32[1,768]{1,0:T(1,128)} %copy.309.bias_ref, bf16[768,1152]{1,0:T(8,128)(2,1)} %slice.220.w_ref, f32[1,1152]{1,0:T(1,128)} %bitcast.301, ...), custom_call_target="tpu_custom_call" | custom-call | flops 1811939328 | bytes 8257536 | tf_op jit(solution)/shard_map/project/pallas_call | solution.py:49
  166.7 7.0 %project.5 = (bf16[1536,768]{1,0:T(8,128)(2,1)}, bf16[1536,768]{1,0:T(8,128)(2,1)}) custom-call(bf16[1536,768]{1,0:T(8,128)(2,1)} %bitcast.256, f32[1,768]{1,0:T(1,128)} %copy.308.gain_ref, f32[1,768]{1,0:T(1,128)} %copy.309.bias_ref, bf16[768,1152]{1,0:T(8,128)(2,1)} %slice.220.w_ref, f32[1,1152]{1,0:T(1,128)} %bitcast.302, ...), custom_call_target="tpu_custom_call" | custom-call | flops 1811939328 | bytes 8257536 | tf_op jit(solution)/shard_map/project/pallas_call | solution.py:49
  173.7 10.8 %attend.3 = (bf16[384,384]{1,0:T(8,128)(2,1)}, f32[3,8,384]{2,1,0:T(8,128)}) custom-call(s32[1]{0:T(128)} %bitcast.47.count_ref, bf16[384,1152]{1,0:T(8,128)(2,1)} %get-tuple-element.40.q_ref.kn_ref.vn_ref, bf16[384,1152]{1,0:T(8,128)(2,1)} %get-tuple-element.40.q_ref.kn_ref.vn_ref, bf16[384,1152]{1,0:T(8,128)(2,1)} %get-tuple-element.40.q_ref.kn_ref.vn_ref, ...), custom_call_target="tpu_custom_call" | custom-call | flops 4076863488 | bytes 3244032 | tf_op jit(solution)/shard_map/attend/pallas_call | solution.py:151
  184.5 11.0 %attend.2 = (bf16[384,384]{1,0:T(8,128)(2,1)}, f32[3,8,384]{2,1,0:T(8,128)}) custom-call(s32[1]{0:T(128)} %bitcast.2.count_ref, bf16[384,1152]{1,0:T(8,128)(2,1)} %get-tuple-element.37.q_ref.kn_ref.vn_ref, bf16[384,1152]{1,0:T(8,128)(2,1)} %get-tuple-element.37.q_ref.kn_ref.vn_ref, bf16[384,1152]{1,0:T(8,128)(2,1)} %get-tuple-element.37.q_ref.kn_ref.vn_ref, ...), custom_call_target="tpu_custom_call" | custom-call | flops 4076863488 | bytes 3244032 | tf_op jit(solution)/shard_map/attend/pallas_call | solution.py:151
  202.7 23.1 %feed_forward.1 = (bf16[384,768]{1,0:T(8,128)(2,1)}, f32[384,768]{1,0:T(8,128)}, bf16[384,768]{1,0:T(8,128)(2,1)}, bf16[768,7040]{1,0:T(8,128)(2,1)}) custom-call(bf16[384,768]{1,0:T(8,128)(2,1)} %bitcast.276, bf16[384,768]{1,0:T(8,128)(2,1)} %bitcast.239, bf16[384,768]{1,0:T(8,128)(2,1)} %bitcast.310, ...), custom_call_target="tpu_custom_call" | custom-call | flops 12230590464 | bytes 25165824 | tf_op jit(solution)/shard_map/feed_forward/pallas_call | solution.py:391
  231.8 17.1 %attend_back.3 = (bf16[1536,768]{1,0:T(8,128)(2,1)}, bf16[384,1152]{1,0:T(8,128)(2,1)}, f32[8,1152]{1,0:T(8,128)}) custom-call(s32[1]{0:T(128)} %bitcast.47.count_ref, bf16[384,1152]{1,0:T(8,128)(2,1)} %get-tuple-element.40.q_ref.kn_ref.vn_ref, bf16[384,1152]{1,0:T(8,128)(2,1)} %get-tuple-element.40.q_ref.kn_ref.vn_ref, ...), custom_call_target="tpu_custom_call" | custom-call | flops 10192158720 | bytes 8257536 | tf_op jit(solution)/shard_map/attend_back/pallas_call | solution.py:278
  248.9 17.6 %attend_back.2 = (bf16[1536,768]{1,0:T(8,128)(2,1)}, bf16[384,1152]{1,0:T(8,128)(2,1)}, f32[8,1152]{1,0:T(8,128)}) custom-call(s32[1]{0:T(128)} %bitcast.2.count_ref, bf16[384,1152]{1,0:T(8,128)(2,1)} %get-tuple-element.37.q_ref.kn_ref.vn_ref, bf16[384,1152]{1,0:T(8,128)(2,1)} %get-tuple-element.37.q_ref.kn_ref.vn_ref, ...), custom_call_target="tpu_custom_call" | custom-call | flops 10192158720 | bytes 8257536 | tf_op jit(solution)/shard_map/attend_back/pallas_call | solution.py:278
  267.7 2.6 fusion.62
  275.5 3.6 fusion.2
  292.9 21.5 %collective-permute-done.20 = bf16[4,2,48,1280]{3,2,1,0:T(8,128)(2,1)S(1)} collective-permute-done((bf16[4,2,48,1280]{3,2,1,0:T(8,128)(2,1)S(1)}, bf16[4,2,48,1280]{3,2,1,0:T(8,128)(2,1)S(1)}, u32[]{:S(2)}, u32[]{:S(2)}) %collective-permute-start.20) | collective-permute-done | bytes 983072 | tf_op jit(solution)/shard_map/ppermute | solution.py:463
  319.9 14.8 %collective-permute-done.21 = bf16[4,48,1280]{2,1,0:T(8,128)(2,1)} collective-permute-done((bf16[4,48,1280]{2,1,0:T(8,128)(2,1)}, bf16[4,48,1280]{2,1,0:T(8,128)(2,1)}, u32[]{:S(2)}, u32[]{:S(2)}) %collective-permute-start.21) | collective-permute-done | bytes 491552 | tf_op jit(solution)/shard_map/ppermute | solution.py:460
  335.9 10.1 %collective-permute-start.22 = (bf16[48,1280]{1,0:T(8,128)(2,1)S(1)}, bf16[48,1280]{1,0:T(8,128)(2,1)S(1)}, u32[]{:S(2)}, u32[]{:S(2)}) collective-permute-start(bf16[48,1280]{1,0:T(8,128)(2,1)S(1)} %get-tuple-element.116), channel_id=1, source_target_pairs={{0,4},{1,5},{2,6},{3,7},{4,8},{5,9},{6,10},{7,11},{8,12},{9,13},{1... | collective-permute-start | bytes 368648 | tf_op jit(solution)/shard_map/ppermute | solution.py:467
  346.0 16.0 %collective-permute-start.23 = (bf16[48,1280]{1,0:T(8,128)(2,1)S(1)}, bf16[48,1280]{1,0:T(8,128)(2,1)S(1)}, u32[]{:S(2)}, u32[]{:S(2)}) collective-permute-start(bf16[48,1280]{1,0:T(8,128)(2,1)S(1)} %get-tuple-element.118), channel_id=1, source_target_pairs={{0,8},{1,9},{2,10},{3,11},{4,12},{5,13},{6,14},{7,15},{8,0},{9,1},... | collective-permute-start | bytes 368648 | tf_op jit(solution)/shard_map/ppermute | solution.py:467
  364.0 2.4 fusion
  368.6 4.1 collective-permute-done.23
  372.7 9.4 %collective-permute-done.24 = bf16[48,1280]{1,0:T(8,128)(2,1)S(1)} collective-permute-done((bf16[48,1280]{1,0:T(8,128)(2,1)S(1)}, bf16[48,1280]{1,0:T(8,128)(2,1)S(1)}, u32[]{:S(2)}, u32[]{:S(2)}) %collective-permute-start.24) | collective-permute-done | bytes 122912 | tf_op jit(solution)/shard_map/ppermute | solution.py:467
  391.4 3.1 collective-permute-done.16
  400.9 2.2 collective-permute-start.19
  407.8 12.1 %collective-permute-done.17 = bf16[2,96,768]{2,1,0:T(8,128)(2,1)S(1)} collective-permute-done((bf16[2,96,768]{2,1,0:T(8,128)(2,1)}, bf16[2,96,768]{2,1,0:T(8,128)(2,1)S(1)}, u32[]{:S(2)}, u32[]{:S(2)}) %collective-permute-start.17) | collective-permute-done | bytes 294944 | tf_op jit(solution)/shard_map/ppermute | solution.py:467
  420.0 3.6 collective-permute-done.18
  423.5 2.5 collective-permute-done.19
  435.7 2.6 reshape.428
  (304 shorter events, 127.4 us)
Async XLA Ops:
  7.2 193.8 %all-gather.2.cloned.1.call-start = ((), (), s32[]{:S(2)}) async-start(), calls=%async_computation.1 | async-start | bytes 11151360 | tf_op jit(solution)/shard_map/all_gather | solution.py:566
  13.5 417.0 %reduce-scatter.4.cloned.1.call-start = ((), (), s32[]{:S(2)}) async-start(), calls=%async_computation.2 | async-start | bytes 11151360
  13.6 58.3 %collective-permute-start.7 = (bf16[2,96,768]{2,1,0:T(8,128)(2,1)S(1)}, bf16[2,96,768]{2,1,0:T(8,128)(2,1)S(1)}, u32[]{:S(2)}, u32[]{:S(2)}) collective-permute-start(bf16[2,96,768]{2,1,0:T(8,128)(2,1)S(1)} %slice_bitcast_fusion.2), channel_id=1, source_target_pairs={{0,4},{1,5},{2,6},{3,7},{4,8},{5,9},{6,10},{7,11},{8,12},{9,13},{1... | collective-permute-start | bytes 884744 | tf_op jit(solution)/shard_map/ppermute | solution.py:467
  15.2 56.8 %collective-permute-start.8 = (bf16[2,96,768]{2,1,0:T(8,128)(2,1)S(1)}, bf16[2,96,768]{2,1,0:T(8,128)(2,1)S(1)}, u32[]{:S(2)}, u32[]{:S(2)}) collective-permute-start(bf16[2,96,768]{2,1,0:T(8,128)(2,1)S(1)} %slice_bitcast_fusion.2), channel_id=1, source_target_pairs={{0,8},{1,9},{2,10},{3,11},{4,12},{5,13},{6,14},{7,15},{8,0},{9,1},... | collective-permute-start | bytes 884744 | tf_op jit(solution)/shard_map/ppermute | solution.py:467
  16.3 55.7 %collective-permute-start.9 = (bf16[2,96,768]{2,1,0:T(8,128)(2,1)S(1)}, bf16[2,96,768]{2,1,0:T(8,128)(2,1)S(1)}, u32[]{:S(2)}, u32[]{:S(2)}) collective-permute-start(bf16[2,96,768]{2,1,0:T(8,128)(2,1)S(1)} %slice_bitcast_fusion.2), channel_id=1, source_target_pairs={{0,12},{1,13},{2,14},{3,15},{4,0},{5,1},{6,2},{7,3},{8,4},{9,5},{1... | collective-permute-start | bytes 884744 | tf_op jit(solution)/shard_map/ppermute | solution.py:467
  18.2 115.7 %collective-permute-start = (bf16[2,2,96,768]{3,2,1,0:T(8,128)(2,1)S(1)}, bf16[2,2,96,768]{3,2,1,0:T(8,128)(2,1)}, u32[]{:S(2)}, u32[]{:S(2)}) collective-permute-start(bf16[2,2,96,768]{3,2,1,0:T(8,128)(2,1)S(1)} %copy-done), channel_id=1, source_target_pairs={{0,1},{1,0},{2,3},{3,2},{4,5},{5,4},{6,7},{7,6},{8,9},{9,8},{10,11... | collective-permute-start | bytes 1769480 | tf_op jit(solution)/shard_map/ppermute | solution.py:457
  19.3 11.4 %collective-permute-start.1 = (bf16[24,1280]{1,0:T(8,128)(2,1)S(1)}, bf16[24,1280]{1,0:T(8,128)(2,1)S(1)}, u32[]{:S(2)}, u32[]{:S(2)}) collective-permute-start(bf16[24,1280]{1,0:T(8,128)(2,1)S(1)} %fusion.44), channel_id=1, source_target_pairs={{0,1},{1,0},{2,3},{3,2},{4,5},{5,4},{6,7},{7,6},{8,9},{9,8},{10,11... | collective-permute-start | bytes 184328 | tf_op jit(solution)/shard_map/ppermute | solution.py:457
  30.7 19.6 %collective-permute-start.2 = (bf16[48,1280]{1,0:T(8,128)(2,1)S(1)}, bf16[48,1280]{1,0:T(8,128)(2,1)S(1)}, u32[]{:S(2)}, u32[]{:S(2)}) collective-permute-start(bf16[48,1280]{1,0:T(8,128)(2,1)S(1)} %bitcast.282), channel_id=1, source_target_pairs={{0,4},{1,5},{2,6},{3,7},{4,8},{5,9},{6,10},{7,11},{8,12},{9,13},{1... | collective-permute-start | bytes 368648 | tf_op jit(solution)/shard_map/ppermute | solution.py:467
  50.3 11.8 %collective-permute-start.3 = (bf16[48,1280]{1,0:T(8,128)(2,1)S(1)}, bf16[48,1280]{1,0:T(8,128)(2,1)S(1)}, u32[]{:S(2)}, u32[]{:S(2)}) collective-permute-start(bf16[48,1280]{1,0:T(8,128)(2,1)S(1)} %bitcast.283), channel_id=1, source_target_pairs={{0,8},{1,9},{2,10},{3,11},{4,12},{5,13},{6,14},{7,15},{8,0},{9,1},... | collective-permute-start | bytes 368648 | tf_op jit(solution)/shard_map/ppermute | solution.py:467
  62.1 8.2 %collective-permute-start.4 = (bf16[48,1280]{1,0:T(8,128)(2,1)S(1)}, bf16[48,1280]{1,0:T(8,128)(2,1)S(1)}, u32[]{:S(2)}, u32[]{:S(2)}) collective-permute-start(bf16[48,1280]{1,0:T(8,128)(2,1)S(1)} %bitcast.285), channel_id=1, source_target_pairs={{0,12},{1,13},{2,14},{3,15},{4,0},{5,1},{6,2},{7,3},{8,4},{9,5},{1... | collective-permute-start | bytes 368648 | tf_op jit(solution)/shard_map/ppermute | solution.py:467
  70.3 14.2 %collective-permute-start.5 = (bf16[4,48,1280]{2,1,0:T(8,128)(2,1)S(1)}, bf16[4,48,1280]{2,1,0:T(8,128)(2,1)S(1)}, u32[]{:S(2)}, u32[]{:S(2)}) collective-permute-start(bf16[4,48,1280]{2,1,0:T(8,128)(2,1)S(1)} %bitcast_dynamic-update-slice_fusion.3), channel_id=1, source_target_pairs={{0,2},{1,3},{2,0},{3,1},{4,6},{5,7},{6,4},{7,5},{8,10},{9,11},{10,... | collective-permute-start | bytes 1474568 | tf_op jit(solution)/shard_map/ppermute | solution.py:460
  72.1 54.2 %collective-permute-start.10 = (bf16[4,2,96,768]{3,2,0,1:T(8,128)(2,1)S(1)}, bf16[4,2,96,768]{3,2,0,1:T(8,128)(2,1)S(1)}, u32[]{:S(2)}, u32[]{:S(2)}) collective-permute-start(bf16[4,2,96,768]{3,2,0,1:T(8,128)(2,1)S(1)} %bitcast_dynamic-update-slice_fusion), channel_id=1, source_target_pairs={{0,2},{1,3},{2,0},{3,1},{4,6},{5,7},{6,4},{7,5},{8,10},{9,11},{10,... | collective-permute-start | bytes 3538952 | tf_op jit(solution)/shard_map/ppermute | solution.py:460
  85.7 51.2 %collective-permute-start.6 = (bf16[4,2,48,1280]{3,2,1,0:T(8,128)(2,1)}, bf16[4,2,48,1280]{3,2,1,0:T(8,128)(2,1)}, u32[]{:S(2)}, u32[]{:S(2)}) collective-permute-start(bf16[4,2,48,1280]{3,2,1,0:T(8,128)(2,1)} %pad_maximum_fusion.3), channel_id=1, source_target_pairs={{0,16},{16,0},{1,17},{17,1},{2,18},{18,2},{3,19},{19,3},{4,20},{20... | collective-permute-start | bytes 2949128 | tf_op jit(solution)/shard_map/ppermute | solution.py:463
  128.0 26.8 %collective-permute-start.11 = (bf16[4,2,2,96,768]{4,3,1,0,2:T(8,128)(2,1)}, bf16[4,2,2,96,768]{4,3,1,0,2:T(8,128)(2,1)}, u32[]{:S(2)}, u32[]{:S(2)}) collective-permute-start(bf16[4,2,2,96,768]{4,3,1,0,2:T(8,128)(2,1)} %pad_maximum_fusion), channel_id=1, source_target_pairs={{0,1},{1,0},{2,3},{3,2},{4,5},{5,4},{6,7},{7,6},{8,9},{9,8},{10,11... | collective-permute-start | bytes 7077896 | tf_op jit(solution)/shard_map/ppermute | solution.py:457
  196.5 1.9 collective-permute-start.12
  228.5 1.7 collective-permute-start.13
  280.8 33.6 %collective-permute-start.20 = (bf16[4,2,48,1280]{3,2,1,0:T(8,128)(2,1)S(1)}, bf16[4,2,48,1280]{3,2,1,0:T(8,128)(2,1)S(1)}, u32[]{:S(2)}, u32[]{:S(2)}) collective-permute-start(bf16[4,2,48,1280]{3,2,1,0:T(8,128)(2,1)S(1)} %fusion.21), channel_id=1, source_target_pairs={{0,16},{16,0},{1,17},{17,1},{2,18},{18,2},{3,19},{19,3},{4,20},{20... | collective-permute-start | bytes 2949128 | tf_op jit(solution)/shard_map/ppermute | solution.py:463
  288.7 75.2 %collective-permute-start.15 = (bf16[4,2,2,96,768]{4,3,2,0,1:T(8,128)(2,1)}, bf16[4,2,2,96,768]{4,3,2,0,1:T(8,128)(2,1)}, u32[]{:S(2)}, u32[]{:S(2)}) collective-permute-start(bf16[4,2,2,96,768]{4,3,2,0,1:T(8,128)(2,1)} %bitcast.236), channel_id=1, source_target_pairs={{0,1},{1,0},{2,3},{3,2},{4,5},{5,4},{6,7},{7,6},{8,9},{9,8},{10,11... | collective-permute-start | bytes 7077896 | tf_op jit(solution)/shard_map/ppermute | solution.py:457
  291.9 22.5 %copy-start.7 = (bf16[768,1152]{1,0:T(8,128)(2,1)S(1)}, bf16[768,1152]{1,0:T(8,128)(2,1)}, u32[]{:S(2)}) copy-start(bf16[768,1152]{1,0:T(8,128)(2,1)} %get-tuple-element.91) | copy-start | bytes 5308420
  292.9 25.7 %collective-permute-start.14 = (bf16[2,2,96,768]{3,2,0,1:T(8,128)(2,1)}, bf16[2,2,96,768]{3,2,0,1:T(8,128)(2,1)}, u32[]{:S(2)}, u32[]{:S(2)}) collective-permute-start(bf16[2,2,96,768]{3,2,0,1:T(8,128)(2,1)} %bitcast.237), channel_id=1, source_target_pairs={{0,1},{1,0},{2,3},{3,2},{4,5},{5,4},{6,7},{7,6},{8,9},{9,8},{10,11... | collective-permute-start | bytes 1769480 | tf_op jit(solution)/shard_map/ppermute | solution.py:457
  316.5 18.2 %collective-permute-start.21 = (bf16[4,48,1280]{2,1,0:T(8,128)(2,1)}, bf16[4,48,1280]{2,1,0:T(8,128)(2,1)}, u32[]{:S(2)}, u32[]{:S(2)}) collective-permute-start(bf16[4,48,1280]{2,1,0:T(8,128)(2,1)} %dynamic-slice_bitcast_fusion.1), channel_id=1, source_target_pairs={{0,2},{1,3},{2,0},{3,1},{4,6},{5,7},{6,4},{7,5},{8,10},{9,11},{10,... | collective-permute-start | bytes 1474568 | tf_op jit(solution)/shard_map/ppermute | solution.py:460
  319.9 62.4 %copy-start.8 = (f32[2,2,96,768]{3,2,0,1:T(8,128)}, f32[2,2,96,768]{3,2,0,1:T(8,128)S(1)}, u32[]{:S(2)}) copy-start(f32[2,2,96,768]{3,2,0,1:T(8,128)S(1)} %convert_add_fusion.3) | copy-start | bytes 3538948
  335.9 32.6 %collective-permute-start.22 = (bf16[48,1280]{1,0:T(8,128)(2,1)S(1)}, bf16[48,1280]{1,0:T(8,128)(2,1)S(1)}, u32[]{:S(2)}, u32[]{:S(2)}) collective-permute-start(bf16[48,1280]{1,0:T(8,128)(2,1)S(1)} %get-tuple-element.116), channel_id=1, source_target_pairs={{0,4},{1,5},{2,6},{3,7},{4,8},{5,9},{6,10},{7,11},{8,12},{9,13},{1... | collective-permute-start | bytes 368648 | tf_op jit(solution)/shard_map/ppermute | solution.py:467
  346.0 26.7 %collective-permute-start.23 = (bf16[48,1280]{1,0:T(8,128)(2,1)S(1)}, bf16[48,1280]{1,0:T(8,128)(2,1)S(1)}, u32[]{:S(2)}, u32[]{:S(2)}) collective-permute-start(bf16[48,1280]{1,0:T(8,128)(2,1)S(1)} %get-tuple-element.118), channel_id=1, source_target_pairs={{0,8},{1,9},{2,10},{3,11},{4,12},{5,13},{6,14},{7,15},{8,0},{9,1},... | collective-permute-start | bytes 368648 | tf_op jit(solution)/shard_map/ppermute | solution.py:467
  362.0 20.1 %collective-permute-start.24 = (bf16[48,1280]{1,0:T(8,128)(2,1)S(1)}, bf16[48,1280]{1,0:T(8,128)(2,1)S(1)}, u32[]{:S(2)}, u32[]{:S(2)}) collective-permute-start(bf16[48,1280]{1,0:T(8,128)(2,1)S(1)} %get-tuple-element.117), channel_id=1, source_target_pairs={{0,12},{1,13},{2,14},{3,15},{4,0},{5,1},{6,2},{7,3},{8,4},{9,5},{1... | collective-permute-start | bytes 368648 | tf_op jit(solution)/shard_map/ppermute | solution.py:467
  367.5 26.9 %collective-permute-start.16 = (bf16[4,2,96,768]{3,2,1,0:T(8,128)(2,1)}, bf16[4,2,96,768]{3,2,1,0:T(8,128)(2,1)}, u32[]{:S(2)}, u32[]{:S(2)}) collective-permute-start(bf16[4,2,96,768]{3,2,1,0:T(8,128)(2,1)} %dynamic-slice_bitcast_fusion), channel_id=1, source_target_pairs={{0,2},{1,3},{2,0},{3,1},{4,6},{5,7},{6,4},{7,5},{8,10},{9,11},{10,... | collective-permute-start | bytes 3538952 | tf_op jit(solution)/shard_map/ppermute | solution.py:460
  382.2 1.4 collective-permute-start.25
  397.1 29.0 %copy-start.9 = (f32[2,2,96,768]{3,2,0,1:T(8,128)S(1)}, f32[2,2,96,768]{3,2,0,1:T(8,128)}, u32[]{:S(2)}) copy-start(f32[2,2,96,768]{3,2,0,1:T(8,128)} %copy-done.8) | copy-start | bytes 3538948
  398.0 22.0 %collective-permute-start.17 = (bf16[2,96,768]{2,1,0:T(8,128)(2,1)}, bf16[2,96,768]{2,1,0:T(8,128)(2,1)S(1)}, u32[]{:S(2)}, u32[]{:S(2)}) collective-permute-start(bf16[2,96,768]{2,1,0:T(8,128)(2,1)} %get-tuple-element.97), channel_id=1, source_target_pairs={{0,4},{1,5},{2,6},{3,7},{4,8},{5,9},{6,10},{7,11},{8,12},{9,13},{1... | collective-permute-start | bytes 884744 | tf_op jit(solution)/shard_map/ppermute | solution.py:467
  399.4 24.1 %collective-permute-start.18 = (bf16[2,96,768]{2,1,0:T(8,128)(2,1)}, bf16[2,96,768]{2,1,0:T(8,128)(2,1)S(1)}, u32[]{:S(2)}, u32[]{:S(2)}) collective-permute-start(bf16[2,96,768]{2,1,0:T(8,128)(2,1)} %get-tuple-element.99), channel_id=1, source_target_pairs={{0,8},{1,9},{2,10},{3,11},{4,12},{5,13},{6,14},{7,15},{8,0},{9,1},... | collective-permute-start | bytes 884744 | tf_op jit(solution)/shard_map/ppermute | solution.py:467
  400.9 25.2 %collective-permute-start.19 = (bf16[2,96,768]{2,1,0:T(8,128)(2,1)S(1)}, bf16[2,96,768]{2,1,0:T(8,128)(2,1)S(1)}, u32[]{:S(2)}, u32[]{:S(2)}) collective-permute-start(bf16[2,96,768]{2,1,0:T(8,128)(2,1)S(1)} %get-tuple-element.98), channel_id=1, source_target_pairs={{0,12},{1,13},{2,14},{3,15},{4,0},{5,1},{6,2},{7,3},{8,4},{9,5},{1... | collective-permute-start | bytes 884744 | tf_op jit(solution)/shard_map/ppermute | solution.py:467
  407.1 20.1 %copy-start.35 = (f32[2,2,96]{2,1,0:T(2,128)S(1)}, f32[2,2,96]{2,1,0:T(2,128)}, u32[]{:S(2)}) copy-start(f32[2,2,96]{2,1,0:T(2,128)} %copy-done.34) | copy-start | bytes 4612
  (43 other events, 234.7 us)
Sparse Core Ops, SparseCore 0:
  13.6 123.4 all-gather.1
  226.0 181.1 reduce-scatter.3
